TPU v7x, 256 devices: a whole 4x4x8 slice. The times are simulated.
256 devices in a mesh: gz: 4 (over x), gy: 64 (over z, y, core).
Axes of the slice: x: 4, y: 4, z: 8, core: 2. Of those that a mesh axis runs over, the one named last changes fastest.
Arguments:
- velocity_x: bfloat16 [8, 1024, 2048], P('gz', 'gy'), may hold values from -1.5 to 1.5
- velocity_y: bfloat16 [8, 1024, 2048], P('gz', 'gy'), may hold values from -1.5 to 1.5
- velocity_z: bfloat16 [8, 1024, 2048], P('gz', 'gy'), may hold values from -1.5 to 1.5
- owners: int32 [512, 1], replicated, may hold values from 0 to 63; in each aligned block of 512 rows (0 to 511, 512 to 1023, ...) at most 16 rows name the same one
- coupling_below: float32 [8], replicated, may hold values from 0.5 to 2
- coupling_above: float32 [8], replicated, may hold values from 0.5 to 2
- metric: float32 [8], replicated, may hold values from 0.25 to 1
Outputs:
- pressure: float32 [64, 16, 2, 8, 1024], P('gy', None, None, 'gz')
Inputs may be any that keep to these rules, and one draw needn't show every extreme that they name: owners[m, 0] is the owner of retained mode kx = m; no owner has more than 16 modes, and some owner has exactly 16.
All inputs are finite; a program needn't handle non-finite values.
Results may differ from a plain program's by a relative error of at most 0.0003.
Values may be sent and summed in bfloat16 or wider, within the bound.
A program may use at most 64 MiB of HBM per device.

v0:
```python
import math

import jax
import jax.numpy as jnp
from jax import lax
from jax.sharding import PartitionSpec as P

CAP = 16


SMAG_COEF = 0.12
STRAIN_FLOOR = 0.01
BASE_SHIFT = 0.004
MODE_SHIFT = 0.02


def with_halo(array, sides, width):
    for axis, dim in sides:
        size, length = (lax.axis_size(axis), array.shape[dim])
        up = [(i, (i + 1) % size) for i in range(size - 1)]
        down = [(j, i) for i, j in up]
        last = lax.slice_in_dim(array, length - width, length, axis=dim)
        leading = lax.slice_in_dim(array, 0, width, axis=dim)
        before = lax.ppermute(last, axis, up)
        after = lax.ppermute(leading, axis, down)
        array = jnp.concatenate([before, array, after], axis=dim)
    return array


def prefix(array, axis, combine, identity, reverse):
    size, here = (lax.axis_size(axis), lax.axis_index(axis))
    everything = jax.tree.map(lambda part: lax.all_gather(part, axis), array)
    start = jax.tree.map(
        lambda part, zero: jnp.broadcast_to(jnp.asarray(zero, part.dtype), part.shape),
        array,
        identity,
    )

    def turn(k, before):
        at = size - 1 - k if reverse else k
        reached = at > here if reverse else at < here
        new = combine(before, jax.tree.map(lambda part: part[at], everything))
        return jax.tree.map(lambda a, b: jnp.where(reached, a, b), new, before)

    return lax.fori_loop(0, size, turn, start)


def shrink(field):
    return field[1:-1, 1:-1]


def centred_x(field):
    return (jnp.roll(field, -1, 2) - jnp.roll(field, 1, 2)) * 0.5


def slope_x(field):
    return shrink(centred_x(field))


def slope_y(field):
    return (field[1:-1, 2:] - field[1:-1, :-2]) * 0.5


def slope_z(field):
    return (field[2:, 1:-1] - field[:-2, 1:-1]) * 0.5


def second_x(field):
    return shrink(jnp.roll(field, -1, 2) + jnp.roll(field, 1, 2) - 2.0 * field)


def second_y(field):
    return field[1:-1, 2:] + field[1:-1, :-2] - 2.0 * shrink(field)


def second_z(field):
    return field[2:, 1:-1] + field[:-2, 1:-1] - 2.0 * shrink(field)


def mixed_yz(field):
    return 0.25 * (field[2:, 2:] - field[2:, :-2] - field[:-2, 2:] + field[:-2, :-2])


def pressure_source(extended):
    slopes = (slope_x, slope_y, slope_z)
    gradient = [
        [slopes[axis_two](extended[axis_one]) for axis_two in range(3)] for axis_one in range(3)
    ]
    strain = {}
    for axis_one in range(3):
        for axis_two in range(axis_one, 3):
            strain[axis_one, axis_two] = 0.5 * (
                gradient[axis_one][axis_two] + gradient[axis_two][axis_one]
            )
    squared = 2.0 * (
        strain[0, 0] * strain[0, 0] + strain[1, 1] * strain[1, 1] + strain[2, 2] * strain[2, 2]
    )
    squared = squared + 4.0 * (
        strain[0, 1] * strain[0, 1] + strain[0, 2] * strain[0, 2] + strain[1, 2] * strain[1, 2]
    )
    viscous = 2.0 * SMAG_COEF * jnp.sqrt(squared + STRAIN_FLOOR)
    stress = {}
    for pair_key in strain:
        stress[pair_key] = viscous * strain[pair_key]
    divergence = shrink(gradient[0][0] + gradient[1][1] + gradient[2][2])
    forcing = second_x(stress[0, 0]) + second_y(stress[1, 1]) + second_z(stress[2, 2])
    crossed = (
        slope_y(centred_x(stress[0, 1])) + slope_z(centred_x(stress[0, 2])) + mixed_yz(stress[1, 2])
    )
    return divergence + forcing + 2.0 * crossed


def slot_table(owners, groups, capacity):
    owner_of = owners[:, 0]
    one_hot = (owner_of[:, None] == jnp.arange(groups, dtype=jnp.int32)[None, :]).astype(jnp.int32)
    before = jnp.cumsum(one_hot, axis=0) - one_hot
    rank_in = jnp.sum(before * one_hot, axis=1)
    slot_of = owner_of * capacity + rank_in
    matches = slot_of[None, :] == jnp.arange(groups * capacity, dtype=jnp.int32)[:, None]
    mode_ids = jnp.arange(owner_of.shape[0], dtype=jnp.int32)
    slot_mode = jnp.sum(jnp.where(matches, mode_ids[None, :], 0), axis=1)
    return (slot_mode, jnp.any(matches, axis=1))


def chain_combine(before_map, after_map):
    first, second = (after_map, before_map)
    p_aa = first[0] * second[0] + first[1] * second[2]
    p_ab = first[0] * second[1] + first[1] * second[3]
    p_ba = first[2] * second[0] + first[3] * second[2]
    p_bb = first[2] * second[1] + first[3] * second[3]
    real_a = first[4] * second[0] + first[5] * second[2] + first[8] * second[4]
    real_b = first[4] * second[1] + first[5] * second[3] + first[8] * second[5]
    imag_a = first[6] * second[0] + first[7] * second[2] + first[8] * second[6]
    imag_b = first[6] * second[1] + first[7] * second[3] + first[8] * second[7]
    factor = first[8] * second[8]
    largest = jnp.maximum(
        jnp.maximum(jnp.abs(p_aa), jnp.abs(p_ab)), jnp.maximum(jnp.abs(p_ba), jnp.abs(p_bb))
    )
    return (
        jnp.stack([p_aa, p_ab, p_ba, p_bb, real_a, real_b, imag_a, imag_b, factor]) / largest[None]
    )


def affine_combine(before_map, after_map):
    return (after_map[0] * before_map[0], after_map[0][:, None] * before_map[1] + after_map[1])


def per_device(velocity_x, velocity_y, velocity_z, owners, coupling_below, coupling_above, metric):
    groups = lax.axis_size("gy")
    depth, rows, width = velocity_x.shape
    kxr = owners.shape[0]
    kyr = 2 * kxr
    levels = coupling_below.shape[0]
    capacity = CAP
    grid_rows = rows * groups
    stacked = jnp.stack([velocity_x, velocity_y, velocity_z])
    extended = with_halo(stacked, (("gz", 1), ("gy", 2)), 2)
    source = pressure_source(extended.astype(jnp.float32))
    norm_factor = 1.0 / math.sqrt(width * grid_rows)
    kx_all = jnp.arange(kxr, dtype=jnp.int32)
    x_cells = jnp.arange(width, dtype=jnp.int32)
    x_phase = jnp.mod(kx_all[:, None] * x_cells[None, :], width).astype(jnp.float32) * (
        2.0 * math.pi / width
    )
    x_table = jnp.stack(
        [jnp.cos(x_phase) * norm_factor, -jnp.sin(x_phase) * norm_factor], axis=1
    ).reshape(2 * kxr, width)
    flat_rows = source.reshape(depth * rows, width)
    spectra = lax.dot_general(
        x_table,
        flat_rows,
        (((1,), (1,)), ((), ())),
        precision=lax.Precision.HIGHEST,
        preferred_element_type=jnp.float32,
    )
    spectra = spectra.reshape(kxr, 2, depth * rows)
    slot_mode, slot_ok = slot_table(owners, groups, capacity)
    outgoing = jnp.take(spectra, slot_mode, axis=0) * slot_ok[:, None, None].astype(jnp.float32)
    outgoing = outgoing.reshape(groups, 1, capacity, 2, depth * rows)
    block_size = min(8, groups)
    turns = groups // block_size
    ky_all = jnp.arange(kyr, dtype=jnp.int32) - kxr
    received = lax.all_to_all(outgoing, "gy", split_axis=0, concat_axis=1, tiled=True)
    items = received.shape[2]
    blocks = received.reshape(turns, block_size, items, 2, depth, rows)

    def one_turn(totals, entry):
        pieces, turn_pos = entry
        y_cells = (turn_pos * block_size + jnp.arange(block_size, dtype=jnp.int32))[
            :, None
        ] * rows + jnp.arange(rows, dtype=jnp.int32)[None, :]
        phases = jnp.mod(y_cells[:, :, None] * ky_all[None, None, :], grid_rows).astype(
            jnp.float32
        ) * (2.0 * math.pi / grid_rows)
        basis = jnp.stack([jnp.cos(phases), jnp.sin(phases)], axis=2)
        product = jnp.einsum("gmrzy,gyjk->mrzjk", pieces, basis, precision=lax.Precision.HIGHEST)
        real_part = product[:, 0, :, 0] + product[:, 1, :, 1]
        imag_part = product[:, 1, :, 0] - product[:, 0, :, 1]
        return (totals + jnp.stack([real_part, imag_part], axis=1), None)

    start = jnp.zeros((items, 2, depth, kyr), jnp.float32)
    totals, _ = lax.scan(one_turn, start, (blocks, jnp.arange(turns, dtype=jnp.int32)))
    own_index = lax.axis_index("gy")
    own_kx = lax.dynamic_slice_in_dim(slot_mode, own_index * capacity, capacity)
    own_ok = lax.dynamic_slice_in_dim(slot_ok, own_index * capacity, capacity)
    radius = own_kx[:, None] * own_kx[:, None] + ky_all[None, :] * ky_all[None, :]
    inside = (radius <= kxr * kxr) & own_ok[:, None]
    kappa = radius.astype(jnp.float32) / float(kxr * kxr)
    rhs = totals * inside[:, None, None, :].astype(jnp.float32)
    layer_ids = jnp.arange(levels, dtype=jnp.int32)
    below_eff = coupling_below * (layer_ids > 0).astype(jnp.float32)
    above_eff = coupling_above * (layer_ids < levels - 1).astype(jnp.float32)
    above_prev = jnp.concatenate([jnp.zeros((1,), jnp.float32), coupling_above[:-1]])
    base_level = lax.axis_index("gz") * depth
    below_raw_own = lax.dynamic_slice_in_dim(coupling_below, base_level, depth)
    above_raw_own = lax.dynamic_slice_in_dim(coupling_above, base_level, depth)
    below_own = lax.dynamic_slice_in_dim(below_eff, base_level, depth)
    above_own = lax.dynamic_slice_in_dim(above_eff, base_level, depth)
    prev_own = lax.dynamic_slice_in_dim(above_prev, base_level, depth)
    metric_own = lax.dynamic_slice_in_dim(metric, base_level, depth)
    diagonals = [
        -(
            below_raw_own[pos]
            + above_raw_own[pos]
            + metric_own[pos] * (BASE_SHIFT + MODE_SHIFT * kappa)
        )
        for pos in range(depth)
    ]
    ones_mode = jnp.ones((capacity, kyr), jnp.float32)
    zeros_mode = jnp.zeros((capacity, kyr), jnp.float32)
    pivots = []
    values = []
    identity = jnp.stack(
        [
            ones_mode,
            zeros_mode,
            zeros_mode,
            ones_mode,
            zeros_mode,
            zeros_mode,
            zeros_mode,
            zeros_mode,
            ones_mode,
        ]
    )
    composite = identity
    for pos in range(depth):
        coupled = below_own[pos] * prev_own[pos] * ones_mode
        level_map = jnp.stack(
            [
                diagonals[pos],
                -coupled,
                ones_mode,
                zeros_mode,
                rhs[:, 0, pos],
                zeros_mode,
                rhs[:, 1, pos],
                zeros_mode,
                -below_own[pos] * ones_mode,
            ]
        )
        composite = chain_combine(composite, level_map)
    incoming = prefix(composite, "gz", chain_combine, identity, False)
    inverse = incoming[2] / incoming[0]
    term = jnp.stack([incoming[4], incoming[6]], axis=1) / incoming[0][:, None]
    for pos in range(depth):
        pivot = diagonals[pos] - below_own[pos] * prev_own[pos] * inverse
        value = rhs[:, :, pos] - below_own[pos] * term
        inverse = 1.0 / pivot
        term = value * inverse[:, None]
        pivots.append(pivot)
        values.append(value)
    alphas = [-above_own[pos] / pivots[pos] for pos in range(depth)]
    betas = [values[pos] / pivots[pos][:, None] for pos in range(depth)]
    back_identity = (ones_mode, jnp.zeros((capacity, 2, kyr), jnp.float32))
    composite = back_identity
    for pos in range(depth - 1, -1, -1):
        composite = affine_combine(composite, (alphas[pos], betas[pos]))
    incoming = prefix(composite, "gz", affine_combine, back_identity, True)
    current = incoming[1]
    solution = [None] * depth
    for pos in range(depth - 1, -1, -1):
        current = alphas[pos][:, None] * current + betas[pos]
        solution[pos] = current
    return jnp.stack(solution, axis=2)[None]


def solution(mesh):
    placed = (P("gz", "gy", None), P("gz", "gy", None), P("gz", "gy", None), P(), P(), P(), P())
    return jax.shard_map(
        per_device,
        mesh=mesh,
        in_specs=placed,
        out_specs=P("gy", None, None, "gz", None),
        check_vma=False,
    )
```

profile of v0, /device:TPU:8, one launch (start us, length us, event | category | flops | bytes accessed | tf_op | source)
XLA Modules:
  0.0 251.5 jit_solution(13285067992595025849)
XLA Ops:
  6.5 1.1 pad_maximum_fusion.6
  7.6 3.4 %collective-permute-start = (bf16[3,2,16,2048]{3,2,1,0:T(8,128)(2,1)S(1)}, bf16[3,2,16,2048]{3,2,1,0:T(8,128)(2,1)S(1)}, u32[]{:S(2)}, u32[]{:S(2)}) collective-permute-start(bf16[3,2,16,2048]{3,2,1,0:T(8,128)(2,1)S(1)} %pad_maximum_fusion.6), channel_id=1, source_target_pairs={{0,64},{64,128},{128,192},{1,65},{65,129},{129,193},{2,66},{66,130... | collective-permute-start | bytes 1179656 | tf_op jit(solution)/shard_map/ppermute | solution.py:24
  11.0 1.3 collective-permute-start.1
  13.1 1.2 reduce-window.6
  26.7 17.9 %negate_multiply_fusion = (f32[512,1,2048]{2,0,1:T(8,128)}, f32[512,1,2048]{2,0,1:T(8,128)}) fusion(), kind=kLoop, calls=%fused_computation.68 | loop fusion | flops 17825792 | bytes 8388608 | tf_op jit(solution)/shard_map/mul | solution.py:166
  44.9 1.9 collective-permute-start.2
  46.9 3.6 %collective-permute-start.3 = (bf16[3,6,2,2048]{3,2,1,0:T(2,128)(2,1)S(1)}, bf16[3,6,2,2048]{3,2,1,0:T(2,128)(2,1)S(1)}, u32[]{:S(2)}, u32[]{:S(2)}) collective-permute-start(bf16[3,6,2,2048]{3,2,1,0:T(2,128)(2,1)S(1)} %get-tuple-element.424), channel_id=1, source_target_pairs={{1,0},{2,1},{3,2},{4,3},{5,4},{6,5},{7,6},{8,7},{9,8},{10,9},{11,1... | collective-permute-start | bytes 442376 | tf_op jit(solution)/shard_map/ppermute | solution.py:25
  54.7 0.9 maximum_convert_fusion
  57.3 3.7 %fusion.44 = (f32[4,18,2048]{2,1,0:T(8,128)S(1)}, f32[4,18,2048]{2,1,0:T(8,128)S(1)}, f32[4,18,2048]{2,1,0:T(8,128)S(1)}, f32[4,18,2048]{2,1,0:T(8,128)S(1)}, f3...) fusion(f32[6,20,2048]{2,1,0:T(8,128)S(1)} %get-tuple-element.40, ...), kind=kLoop, calls=%fused_computation.117 | loop fusion | flops 7372800 | bytes 17694720 | tf_op jit(solution)/shard_map/mul | solution.py:104
  64.0 1.2 copy-done.1
  65.2 1.4 copy-done
  66.5 7.7 %fusion.15 = f32[512,2,32]{0,2,1:T(8,128)S(1)} fusion(f32[32,2048,1]{1,0,2:T(8,128)S(1)} %bitcast.327, f32[512,1,2048]{2,0,1:T(8,128)S(1)} %copy-done, f32[512,1,2048]{2,0,1:T(8,128)S(1)} %copy-done.1), kind=kOutput, calls=%fused_computation.58 | convolution fusion | flops 807403520 | bytes 8781824 | tf_op jit(solution)/shard_map/dot_general | solution.py:169
  74.5 3.5 %gather_fusion = f32[1024,2,32]{2,1,0:T(2,128)S(1)} fusion(f32[512,2,32]{2,1,0:T(2,128)S(1)} %copy.61, s32[1024]{0:T(1024)S(1)} %broadcast_clamp_fusion), kind=kCustom, calls=%fused_computation | custom fusion | bytes 528384 | tf_op jit(solution)/shard_map/jit(_take)/gather | solution.py:178
  78.5 1.2 reshape.1083
  79.6 13.8 %all-to-all-start = ((f32[64,1,1024]{2,1,0:T(1,128)}), f32[64,1,1024]{2,1,0:T(1,128)S(1)}, u32[]{:S(2)}, u32[]{:S(2)}) async-start(f32[64,1,1024]{2,1,0:T(1,128)} %reshape.1083), calls=%async_computation | async-start | bytes 524288 | tf_op jit(solution)/shard_map/all_to_all | solution.py:183
  94.3 11.3 %all-to-all-done = f32[64,1,1024]{2,1,0:T(1,128)S(1)} async-done(((f32[64,1,1024]{2,1,0:T(1,128)}), f32[64,1,1024]{2,1,0:T(1,128)S(1)}, u32[]{:S(2)}, u32[]{:S(2)}) %all-to-all-start) | async-done | bytes 262176 | tf_op jit(solution)/shard_map/all_to_all | solution.py:183
  106.1 1.3 reduce.2
  107.4 1.3 reshape.1084
  108.7 2.5 reshape.1068
  111.2 39.6 %while.43 = (s32[]{:T(128)}, f32[16,2,2,1024]{3,0,2,1:T(8,128)S(1)}, f32[8,8,16,2,2,16]{5,4,2,3,1,0:T(2,128)S(1)}, s32[8]{0:T(128)S(1)}, s32[]{:T(128)}, /*index=5*/s32[1]{0:T(128)}, s32[]{:T(128)}) while((s32[]{:T(128)}, f32[16,2,2,1024]{3,0,2,1:T(8,128)S(1)}, f32[8,8,16,2,2,16]{5,4,2,3,1,0:T(2,128)S(1)}, s32[8]{0:T(128)S(1)}, ...), condition=%wide.region_6.7_spmd.clone, body=%wide.region_5.6_spmd.clone.sunk | while | flops 203687056 | bytes 4302007 | solution.py:202
  112.6 2.1 fusion.141
  114.7 1.3 convolution_bitcast_fusion.2
  117.5 2.1 fusion.141
  119.7 1.3 convolution_bitcast_fusion.2
  122.5 2.1 fusion.141
  124.6 1.3 convolution_bitcast_fusion.2
  127.4 2.1 fusion.141
  129.6 1.3 convolution_bitcast_fusion.2
  132.4 2.1 fusion.141
  134.5 1.3 convolution_bitcast_fusion.2
  137.3 2.1 fusion.141
  139.5 1.3 convolution_bitcast_fusion.2
  142.3 2.1 fusion.141
  144.4 1.3 convolution_bitcast_fusion.2
  147.2 2.1 fusion.141
  149.4 1.3 convolution_bitcast_fusion.2
  156.6 31.1 %all-gather.2.cloned.1.call-done = f32[4,9,16,1024]{3,2,1,0:T(8,128)} async-done(((f32[1,9,16,1024]{3,2,1,0:T(8,128)}), f32[4,9,16,1024]{3,2,1,0:T(8,128)}) %all-gather.2.cloned.1.call-update) | async-done | bytes 2359312 | tf_op jit(solution)/shard_map/all_gather | solution.py:32
  187.7 23.3 %while.42 = (s32[]{:T(128)}, f32[9,16,1024]{2,1,0:T(8,128)S(1)}, s32[]{:T(128)}, f32[4,9,16,1024]{3,2,1,0:T(8,128)}, s32[]{:T(128)}, /*index=5*/s32[]{:T(128)}, ...) while((s32[]{:T(128)}, f32[9,16,1024]{2,1,0:T(8,128)S(1)}, s32[]{:T(128)}, ...), condition=%wide.region_8.9_spmd, body=%wide.region_7.8_spmd.sunk | while | flops 950283 | bytes 5243207 | solution.py:45
  187.7 1.0 maximum_bitcast_fusion.7
  188.8 0.9 add_dynamic-update-slice_fusion.10
  189.7 0.9 add_dynamic-update-slice_fusion.11
  190.6 0.9 add_dynamic-update-slice_fusion.12
  191.6 0.9 add_dynamic-update-slice_fusion.13
  193.5 1.0 maximum_bitcast_fusion.7
  194.6 0.9 add_dynamic-update-slice_fusion.10
  195.5 0.9 add_dynamic-update-slice_fusion.11
  196.5 0.9 add_dynamic-update-slice_fusion.12
  197.4 0.9 add_dynamic-update-slice_fusion.13
  199.4 1.0 maximum_bitcast_fusion.7
  200.4 0.9 add_dynamic-update-slice_fusion.10
  201.3 0.9 add_dynamic-update-slice_fusion.11
  202.3 0.9 add_dynamic-update-slice_fusion.12
  203.2 0.9 add_dynamic-update-slice_fusion.13
  205.2 1.0 maximum_bitcast_fusion.7
  206.2 0.9 add_dynamic-update-slice_fusion.10
  207.2 0.9 add_dynamic-update-slice_fusion.11
  208.1 0.9 add_dynamic-update-slice_fusion.12
  209.0 0.9 add_dynamic-update-slice_fusion.13
  211.7 1.4 slice_bitcast_fusion.10
  214.0 1.3 fusion.72
  215.2 13.5 %all_gather.14 = f32[4,16,2,1024]{3,1,2,0:T(8,128)S(1)} all-gather(f32[1,16,2,1024]{3,1,2,0:T(8,128)S(1)} %fusion.72), channel_id=1, replica_groups=mesh['gz'=4,'gy'=64] {'gz'}, dimensions={0}, use_global_device_ids=true | all-gather | bytes 655360 | tf_op jit(solution)/shard_map/all_gather | solution.py:32
  228.7 12.5 %all_gather.13 = f32[4,16,1024]{2,1,0:T(8,128)S(1)} all-gather(f32[1,16,1024]{2,1,0:T(8,128)S(1)} %get-tuple-element.443), channel_id=1, replica_groups=mesh['gz'=4,'gy'=64] {'gz'}, dimensions={0}, use_global_device_ids=true | all-gather | bytes 327680 | tf_op jit(solution)/shard_map/all_gather | solution.py:32
  241.2 1.2 while.44
  242.4 1.3 add_bitcast_fusion
  (203 shorter events, 36.2 us)
Async XLA Ops:
  7.6 37.0 %collective-permute-start = (bf16[3,2,16,2048]{3,2,1,0:T(8,128)(2,1)S(1)}, bf16[3,2,16,2048]{3,2,1,0:T(8,128)(2,1)S(1)}, u32[]{:S(2)}, u32[]{:S(2)}) collective-permute-start(bf16[3,2,16,2048]{3,2,1,0:T(8,128)(2,1)S(1)} %pad_maximum_fusion.6), channel_id=1, source_target_pairs={{0,64},{64,128},{128,192},{1,65},{65,129},{129,193},{2,66},{66,130... | collective-permute-start | bytes 1179656 | tf_op jit(solution)/shard_map/ppermute | solution.py:24
  11.0 33.6 %collective-permute-start.1 = (bf16[3,2,16,2048]{3,2,1,0:T(8,128)(2,1)S(1)}, bf16[3,2,16,2048]{3,2,1,0:T(8,128)(2,1)S(1)}, u32[]{:S(2)}, u32[]{:S(2)}) collective-permute-start(bf16[3,2,16,2048]{3,2,1,0:T(8,128)(2,1)S(1)} %pad_maximum_fusion.6), channel_id=1, source_target_pairs={{64,0},{128,64},{192,128},{65,1},{129,65},{193,129},{66,2},{130,66... | collective-permute-start | bytes 1179656 | tf_op jit(solution)/shard_map/ppermute | solution.py:25
  26.7 18.0 %copy-start.2 = (bf16[2,16,2048]{2,1,0:T(8,128)(2,1)S(1)}, bf16[2,16,2048]{2,1,0:T(8,128)(2,1)}, u32[]{:S(2)}) copy-start(bf16[2,16,2048]{2,1,0:T(8,128)(2,1)} %param.15) | copy-start | bytes 393220
  26.7 18.0 %copy-start.3 = (bf16[2,16,2048]{2,1,0:T(8,128)(2,1)S(1)}, bf16[2,16,2048]{2,1,0:T(8,128)(2,1)}, u32[]{:S(2)}) copy-start(bf16[2,16,2048]{2,1,0:T(8,128)(2,1)} %param.14) | copy-start | bytes 393220
  26.7 18.0 %copy-start.4 = (bf16[2,16,2048]{2,1,0:T(8,128)(2,1)S(1)}, bf16[2,16,2048]{2,1,0:T(8,128)(2,1)}, u32[]{:S(2)}) copy-start(bf16[2,16,2048]{2,1,0:T(8,128)(2,1)} %param.13) | copy-start | bytes 393220
  44.9 9.7 %collective-permute-start.2 = (bf16[3,6,2,2048]{3,2,1,0:T(2,128)(2,1)S(1)}, bf16[3,6,2,2048]{3,2,1,0:T(2,128)(2,1)S(1)}, u32[]{:S(2)}, u32[]{:S(2)}) collective-permute-start(bf16[3,6,2,2048]{3,2,1,0:T(2,128)(2,1)S(1)} %get-tuple-element.423), channel_id=1, source_target_pairs={{0,1},{1,2},{2,3},{3,4},{4,5},{5,6},{6,7},{7,8},{8,9},{9,10},{10,1... | collective-permute-start | bytes 442376 | tf_op jit(solution)/shard_map/ppermute | solution.py:24
  46.9 7.8 %collective-permute-start.3 = (bf16[3,6,2,2048]{3,2,1,0:T(2,128)(2,1)S(1)}, bf16[3,6,2,2048]{3,2,1,0:T(2,128)(2,1)S(1)}, u32[]{:S(2)}, u32[]{:S(2)}) collective-permute-start(bf16[3,6,2,2048]{3,2,1,0:T(2,128)(2,1)S(1)} %get-tuple-element.424), channel_id=1, source_target_pairs={{1,0},{2,1},{3,2},{4,3},{5,4},{6,5},{7,6},{8,7},{9,8},{10,9},{11,1... | collective-permute-start | bytes 442376 | tf_op jit(solution)/shard_map/ppermute | solution.py:25
  63.0 2.2 copy-start.1
  63.3 3.2 %copy-start = (f32[512,1,2048]{2,0,1:T(8,128)S(1)}, f32[512,1,2048]{2,0,1:T(8,128)}, u32[]{:S(2)}) copy-start(f32[512,1,2048]{2,0,1:T(8,128)} %get-tuple-element.467) | copy-start | bytes 12582916
  79.6 26.0 %all-to-all-start = ((f32[64,1,1024]{2,1,0:T(1,128)}), f32[64,1,1024]{2,1,0:T(1,128)S(1)}, u32[]{:S(2)}, u32[]{:S(2)}) async-start(f32[64,1,1024]{2,1,0:T(1,128)} %reshape.1083), calls=%async_computation | async-start | bytes 524288 | tf_op jit(solution)/shard_map/all_to_all | solution.py:183
  93.4 94.3 %all-gather.2.cloned.1.call-start = ((), (), s32[]{:S(2)}) async-start(), calls=%async_computation.1 | async-start | bytes 2949120 | tf_op jit(solution)/shard_map/all_gather | solution.py:32
  151.1 3.5 %copy-start.5 = (f32[8]{0:T(128)S(1)}, f32[8]{0:T(128)}, u32[]{:S(2)}) copy-start(f32[8]{0:T(128)} %param.18) | copy-start | bytes 100
Sparse Core Ops, SparseCore 0:
  154.7 33.0 all-gather.1
where the time goes:
time: 253 us; the launch traced here: 251 us
  other arithmetic  86.3 us (34%)
  waiting for transfers between devices  42.5 us (17%)
  local copies, waits for them, and re-layouts  26.8 us (11%)
  blocking collectives  25.9 us (10%)
  starting transfers between devices  24.1 us (10%)
  between operations  21.5 us (8%)
  matrix products  18.2 us (7%)
  loops' own time  6.17 us (2%)
    all_gather x1, waiting for transfers between devices, prefix(): everything = jax.tree.map(lambda part: lax.all_gather(part, axis), array)  31.1 us
    all_gather x2, blocking collectives, prefix(): everything = jax.tree.map(lambda part: lax.all_gather(part, axis), array)  25.9 us
    mul x1, other arithmetic, per_device(): -jnp.sin(x_phase) * norm_factor  17.9 us
    cos x8, other arithmetic, one_turn(): basis = jnp.stack([jnp.cos(phases), jnp.sin(phases)], axis=2)  16.9 us
    while x16, other arithmetic  15 us
    all_to_all x1, starting transfers between devices, per_device(): lax.all_to_all(outgoing, 'gy', split_axis=0, concat_axis=1, tiled=True)  13.8 us
    all_to_all x1, waiting for transfers between devices, per_device(): lax.all_to_all(outgoing, 'gy', split_axis=0, concat_axis=1, tiled=True)  11.3 us
    dot_general x8, matrix products, one_turn(): jnp.einsum('gmrzy,gyjk->mrzjk', pieces, basis, precision=lax.Precision.HI...  10.5 us
  transfers between devices with their start and end apart: 6, of which 2 were waited for; matrix products, arithmetic and copies ran while one was open for 13% of the time, Pallas kernels for 0%

commit v1 on v0

v1 whole, which is shorter than its diff:
```python
import functools
import math

import jax
import jax.numpy as jnp
import ml_dtypes
import numpy as np
from jax import lax
from jax.experimental import pallas as pl
from jax.experimental.pallas import tpu as pltpu
from jax.sharding import PartitionSpec as P

MESH = pl.DeviceIdType.MESH
F32, BF16, I32 = jnp.float32, jnp.bfloat16, jnp.int32
SMAG_COEF = 0.12
STRAIN_FLOOR = 0.01
BASE_SHIFT = 0.004
MODE_SHIFT = 0.02
NX, NY, NZ, KXR, CAP = 2048, 1024, 8, 512, 16
NGZ, NGY = 4, 64
DEPTH, ROWS = 2, 16
DIAGONAL = ((1, 1), (1, -1), (-1, 1), (-1, -1))


def halves(table):
    high = table.astype(ml_dtypes.bfloat16)
    low = (table - high.astype(np.float64)).astype(ml_dtypes.bfloat16)
    return high, low


def tables():
    a = np.arange(16)
    first = np.zeros((16, 16))
    first[0], first[1] = 1.0, (-1.0) ** a
    for r in range(1, 8):
        first[2 * r] = np.cos(2 * np.pi * ((r * a) % 16) / 16)
        first[2 * r + 1] = -np.sin(2 * np.pi * ((r * a) % 16) / 16)
    spread = np.einsum("ca,rs->crsa", first, np.eye(16)).reshape(256, 256)
    x_first = np.stack(halves(spread))

    b = np.arange(128)
    q = np.arange(32)
    second = np.zeros((8, 2, 128, 2, 2, 32))
    for i in range(8):
        for which, r in enumerate((i, 8 if i == 0 else 16 - i)):
            angle = 2 * np.pi * ((b[:, None] * (16 * q[None, :] + r)) % NX) / NX
            c, s = np.cos(angle), np.sin(angle)
            if i == 0:
                second[i, which, :, 0, which] = c
                second[i, which, :, 1, which] = -s
            else:
                sign = 1.0 if which == 0 else -1.0
                second[i, 0, :, 0, which] = c
                second[i, 1, :, 0, which] = sign * s
                second[i, 0, :, 1, which] = -s
                second[i, 1, :, 1, which] = sign * c
    second = second.reshape(8, 256, 128) / math.sqrt(NX * NY)
    x_second = np.concatenate(halves(second), axis=2)

    s64 = np.arange(64)
    angle = 2 * np.pi * ((s64[:, None] * s64[None, :]) % 64) / 64
    c, s = np.cos(angle), np.sin(angle)
    y_first = np.concatenate([np.concatenate([c, -s], 1), np.concatenate([s, c], 1)], 0)
    y_first = np.concatenate(halves(y_first), axis=1)

    j = np.arange(16)
    angle = 2 * np.pi * (j[:, None] * s64[None, :]) / NY
    c, s = np.cos(angle), np.sin(angle)
    turn = np.stack([np.concatenate([c, c], 1), np.concatenate([s, -s], 1)]).astype(np.float32)

    angle = 2 * np.pi * ((j[:, None] * j[None, :]) % 16) / 16
    both = np.stack([np.cos(angle), np.sin(angle)])
    spread = np.einsum("pqj,xu,yv->pqxyvuj", both, np.eye(2), np.eye(8)).reshape(512, 256)
    y_second = np.concatenate(halves(spread), axis=0)
    return x_first, x_second, y_first, turn, y_second


def split(value):
    high = value.astype(BF16)
    return high, (value - high.astype(F32)).astype(BF16)


def dot(left, right):
    return jnp.dot(left, right, preferred_element_type=F32)


def mode_of(position):
    block, which, q = position // 64, (position // 32) % 2, position % 32
    r = jnp.where(which == 0, block, jnp.where(block == 0, 8, 16 - block))
    return 16 * q + r


def iota(shape, dim):
    return lax.broadcasted_iota(I32, shape, dim)


def next_x(field, ahead):
    if ahead:
        turned = pltpu.roll(field, 127, 2)
        return jnp.where(iota(field.shape, 2) == 127, pltpu.roll(turned, 15, 1), turned)
    turned = pltpu.roll(field, 1, 2)
    return jnp.where(iota(field.shape, 2) == 0, pltpu.roll(turned, 1, 1), turned)


def kernel(
    vx, vy, vz, owners, below, above, metric, x_first_in, x_second_in, y_first_in, turn_in,
    y_second_in, out,
    own, spread, ext, stress, source, outgoing, received, x_first, x_second, y_first, turn,
    y_second, chosen, pivots, edges, edge_in, spectrum,
    in_sem, halo_send, halo_recv, all_send, all_recv, edge_send, edge_recv, own_sem,
):
    gz, gy = lax.axis_index("gz"), lax.axis_index("gy")

    def peer(dz, dy):
        return (lax.rem(gz + dz + NGZ, NGZ), lax.rem(gy + dy + NGY, NGY))

    loads = [pltpu.make_async_copy(v, own.at[i], in_sem.at[i]) for i, v in enumerate((vx, vy, vz))]
    for index, (given, kept) in enumerate(
        ((x_first_in, x_first), (x_second_in, x_second), (y_first_in, y_first), (turn_in, turn),
         (y_second_in, y_second))
    ):
        loads.append(pltpu.make_async_copy(given, kept, in_sem.at[3 + index]))
    for load in loads:
        load.start()

    barrier = pltpu.get_barrier_semaphore()

    @pl.loop(1, NGY)
    def _(d):
        pl.semaphore_signal(barrier, inc=1, device_id=peer(0, d), device_id_type=MESH)

    for d in range(1, NGZ):
        pl.semaphore_signal(barrier, inc=1, device_id=peer(d, 0), device_id_type=MESH)
    for dz, dy in DIAGONAL:
        pl.semaphore_signal(barrier, inc=1, device_id=peer(dz, dy), device_id_type=MESH)

    for c in range(3):
        loads[c].wait()
    for c in range(3):
        for z in range(DEPTH):
            base = (c * DEPTH + z) * ROWS * 16
            for a in range(16):
                spread[pl.ds(base + a, 16, stride=16), :] = own[
                    c, z, :, a * 128 : (a + 1) * 128
                ].astype(F32)
            ext[c, z + 2, 2:18] = spread[base : base + 256, :].reshape(16, 16, 128).astype(BF16)

    pl.semaphore_wait(barrier, NGY - 1 + NGZ - 1 + len(DIAGONAL))

    def level_span(dz):
        return pl.ds({1: 0, 0: 2, -1: 4}[dz], 2)

    def halo(index, dz, dy, levels_from, levels_to):
        rows_from = pl.ds({1: 16, 0: 2, -1: 2}[dy], 16 if dy == 0 else 2)
        rows_to = pl.ds({1: 0, 0: 2, -1: 18}[dy], 16 if dy == 0 else 2)
        return pltpu.make_async_remote_copy(
            src_ref=ext.at[:, levels_from, rows_from],
            dst_ref=ext.at[:, levels_to, rows_to],
            send_sem=halo_send.at[index],
            recv_sem=halo_recv.at[index],
            device_id=peer(dz, dy),
            device_id_type=MESH,
        )

    near = [
        halo(0, 1, 0, pl.ds(3, 1), pl.ds(1, 1)),
        halo(1, -1, 0, pl.ds(2, 1), pl.ds(4, 1)),
        halo(2, 0, 1, level_span(0), level_span(0)),
        halo(3, 0, -1, level_span(0), level_span(0)),
    ]
    for index, (dz, dy) in enumerate(DIAGONAL):
        near.append(halo(4 + index, dz, dy, level_span(0), level_span(dz)))
    far = [halo(8, 1, 0, pl.ds(2, 1), pl.ds(0, 1)), halo(9, -1, 0, pl.ds(3, 1), pl.ds(5, 1))]
    for copy in near + far:
        copy.start()

    owner_row = owners[...]
    kx_row = mode_of(iota((1, KXR), 1))
    named = jnp.where(owner_row == iota((NGY, KXR), 0), 1.0, 0.0).astype(BF16)
    place = jnp.where(iota((KXR, KXR), 0) == kx_row, 1.0, 0.0).astype(BF16)
    named = dot(named, place)
    smaller = jnp.where(mode_of(iota((KXR, 1), 0)) < kx_row, 1.0, 0.0).astype(BF16)
    rank = dot(named.astype(BF16), smaller)
    slot_row = jnp.sum(
        named * (rank + CAP * iota((NGY, KXR), 0).astype(F32)), axis=0, keepdims=True
    ).astype(I32)
    for chi in range(2):
        m = iota((512, 1), 0)
        slot_id = (m // 8) * CAP + chi * 8 + m % 8
        chosen[chi] = jnp.where(slot_row == slot_id, 1.0, 0.0).astype(BF16)
    mine = slot_row == gy * CAP + iota((CAP, KXR), 0)
    own_kx = jnp.sum(jnp.where(mine, kx_row.astype(F32), 0.0), axis=1, keepdims=True)
    own_ok = jnp.sum(jnp.where(mine, 1.0, 0.0), axis=1, keepdims=True)
    ky = (iota((1, NY), 1) - KXR).astype(F32)
    radius = own_kx * own_kx + ky * ky
    inside = jnp.where(radius <= float(KXR * KXR), 1.0, 0.0) * own_ok

    shift = BASE_SHIFT + MODE_SHIFT * (radius / float(KXR * KXR))
    for k in range(NZ):
        pivot = -(below[k] + above[k] + metric[k] * shift)
        if k > 0:
            pivot = pivot - below[k] * above[k - 1] * pivots[2, k - 1]
        pivots[0, k] = pivot
        pivots[2, k] = 1.0 / pivot
    for k in range(NZ - 1, -1, -1):
        pivot = -(below[k] + above[k] + metric[k] * shift)
        if k < NZ - 1:
            pivot = pivot - above[k] * below[k + 1] * pivots[3, k + 1]
        pivots[1, k] = pivot
        pivots[3, k] = 1.0 / pivot

    def zero_rim(levels):
        @pl.when(gy == 0)
        def _():
            for level in levels:
                ext[:, level, 0:2] = jnp.zeros((3, 2, 16, 128), BF16)

        @pl.when(gy == NGY - 1)
        def _():
            for level in levels:
                ext[:, level, 18:20] = jnp.zeros((3, 2, 16, 128), BF16)

    def zero_level(edge, level):
        @pl.when(gz == edge)
        def _():
            for c in range(3):
                ext[c, level] = jnp.zeros((20, 16, 128), BF16)

    def at(c, level, row, count):
        return ext[c, level, pl.ds(row, count)].astype(F32)

    def stress_rows(level, wanted, row, count):
        centre = [at(c, level, row, count) for c in range(3)]
        grad = []
        for c in range(3):
            dx = (next_x(centre[c], True) - next_x(centre[c], False)) * 0.5
            dy = (at(c, level, row + 1, count) - at(c, level, row - 1, count)) * 0.5
            dz = (at(c, level + 1, row, count) - at(c, level - 1, row, count)) * 0.5
            grad.append((dx, dy, dz))
        strain = {
            (i, j): grad[i][i] if i == j else 0.5 * (grad[i][j] + grad[j][i])
            for i in range(3) for j in range(i, 3)
        }
        squared = 2.0 * sum(strain[i, i] * strain[i, i] for i in range(3))
        squared = squared + 4.0 * sum(
            strain[i, j] * strain[i, j] for i in range(3) for j in range(i + 1, 3)
        )
        viscous = 2.0 * SMAG_COEF * jnp.sqrt(squared + STRAIN_FLOOR)
        for index, pair in enumerate(((2, 2), (0, 2), (1, 2), (0, 0), (0, 1), (1, 1))):
            if index < wanted:
                stress[index, level - 1, pl.ds(row - 1, count)] = viscous * strain[pair]

    for copy in near:
        copy.wait_recv()
    zero_level(0, 1)
    zero_level(NGZ - 1, 4)
    zero_rim((1, 2, 3, 4))

    @pl.loop(0, 18)
    def _(step):
        stress_rows(2 + step // 9, 6, 1 + 2 * lax.rem(step, 9), 2)

    for copy in far:
        copy.wait_recv()
    zero_level(0, 0)
    zero_level(NGZ - 1, 5)
    zero_rim((0, 5))

    @pl.loop(0, 18)
    def _(step):
        stress_rows(1 + 3 * (step // 9), 3, 1 + 2 * lax.rem(step, 9), 2)

    for z in range(DEPTH):

        @pl.loop(0, 8)
        def _(step):
            row = 2 * step

            def part(index, dz, dy):
                return stress[index, z + 1 + dz, pl.ds(row + 1 + dy, 2)]

            def wind(c, dz, dy):
                return at(c, z + 2 + dz, row + 2 + dy, 2)

            total = 0.5 * (wind(1, 0, 1) - wind(1, 0, -1) + wind(2, 1, 0) - wind(2, -1, 0))
            total = total + part(5, 0, 1) + part(5, 0, -1) + part(0, 1, 0) + part(0, -1, 0)
            total = total - 2.0 * (part(3, 0, 0) + part(5, 0, 0) + part(0, 0, 0))
            total = total + 0.5 * (
                part(2, 1, 1) - part(2, 1, -1) - part(2, -1, 1) + part(2, -1, -1)
            )
            odd = 0.5 * (
                wind(0, 0, 0) + part(4, 0, 1) - part(4, 0, -1) + part(1, 1, 0) - part(1, -1, 0)
            )
            even = part(3, 0, 0)
            total = total + next_x(even + odd, True) + next_x(even - odd, False)
            high, low = split(total.reshape(32, 128))
            start = pl.multiple_of(32 * step, 32)
            source[0, pl.ds(start, 32), z * 128 : (z + 1) * 128] = high
            source[1, pl.ds(start, 32), z * 128 : (z + 1) * 128] = low

    for load in loads[3:]:
        load.wait()
    high, low = source[0], source[1]
    first = dot(x_first[0], high) + dot(x_first[0], low) + dot(x_first[1], high)
    parts = []
    for i in range(8):
        rows = first[32 * i : 32 * i + 32]
        left = jnp.concatenate(
            [
                jnp.concatenate([rows[0:16, 128 * z : 128 * z + 128], rows[16:32, 128 * z : 128 * z + 128]], 1)
                for z in range(DEPTH)
            ],
            0,
        )
        high, low = split(left)
        both = dot(jnp.concatenate([high, low], 0), x_second[i])
        value = both[0:32, 0:128] + both[32:64, 0:128] + both[0:32, 128:256]
        parts.append(value)
    pieces = []
    for i in range(0, 8, 2):
        one, two = parts[i], parts[i + 1]
        front = iota((32, 128), 1) < 64
        real = jnp.where(front, one, pltpu.roll(two, 64, 1))
        imag = jnp.where(front, pltpu.roll(one, 64, 1), two)
        pieces.append(jnp.concatenate([real, imag], 0))
    modes = jnp.concatenate(pieces, 1)
    high, low = split(modes)
    modes = jnp.concatenate([high, low], 0)
    slots = []
    for chi in range(2):
        taken = lax.dot_general(
            chosen[chi], modes, (((1,), (1,)), ((), ())), preferred_element_type=F32
        )
        slots.append(taken + pltpu.roll(taken, 64, 1))
    together = jnp.where(iota((512, 128), 1) < 64, slots[0], slots[1])
    outgoing[...] = together.reshape(NGY, 8, 128)

    def exchange(d):
        there = lax.rem(gy + d, NGY)
        return pltpu.make_async_remote_copy(
            src_ref=outgoing.at[there],
            dst_ref=received.at[gy],
            send_sem=all_send.at[d],
            recv_sem=all_recv.at[d],
            device_id=(gz, there),
            device_id_type=MESH,
        )

    @pl.loop(1, NGY)
    def _(d):
        exchange(d).start()

    keep = pltpu.make_async_copy(outgoing.at[gy], received.at[gy], own_sem)
    keep.start()
    for copy in near + far:
        copy.wait_send()
    keep.wait()

    @pl.loop(1, NGY)
    def _(d):
        exchange(d).wait()

    rows = []
    flat = received.reshape(NGY * 8, 128)
    for clo in range(8):
        turned = flat[pl.ds(clo, NGY, stride=8), :].T
        for chi in range(2):
            real, imag = turned[64 * chi : 64 * chi + 32], turned[64 * chi + 32 : 64 * chi + 64]
            rows.append(jnp.concatenate([real, imag], 1))
    left = jnp.concatenate(rows, 0)
    high, low = split(left)
    both = dot(jnp.concatenate([high, low], 0), y_first[...])
    value = both[0:512, 0:128] + both[512:1024, 0:128] + both[0:512, 128:256]
    value = value.reshape(32, 16, 128)
    swapped = pltpu.roll(value, 64, 2)
    value = (value * turn[0] + swapped * turn[1]).reshape(16, 2, 16, 128)
    right = jnp.concatenate([value[:, z].reshape(256, 128) for z in range(DEPTH)], 1)
    high, low = split(right)
    by_high = dot(y_second[...], high)
    by_low = dot(y_second[0:512], low)
    both = by_high[0:512] + by_high[512:1024] + by_low
    sign = jnp.where(iota((256, 128), 1) < 64, 1.0, -1.0)
    for z in range(DEPTH):
        lanes = slice(128 * z, 128 * z + 128)
        value = both[0:256, lanes] + pltpu.roll(both[256:512, lanes], 64, 1) * sign
        front = iota((16, 128), 1) < 64
        for pair in range(8):
            one, two = value[32 * pair : 32 * pair + 16], value[32 * pair + 16 : 32 * pair + 32]
            where = slice(128 * ((pair + 4) % 8), 128 * ((pair + 4) % 8) + 128)
            kept = inside[:, where]
            spectrum[0, z, :, where] = jnp.where(front, one, pltpu.roll(two, 64, 1)) * kept
            spectrum[1, z, :, where] = jnp.where(front, pltpu.roll(one, 64, 1), two) * kept

    low_level, high_level = DEPTH * gz, DEPTH * gz + 1
    up = below[high_level] * pivots[2, low_level]
    down = above[low_level] * pivots[3, high_level]
    for part in range(2):
        edges[0, part] = spectrum[part, 1] - up * spectrum[part, 0]
        edges[1, part] = spectrum[part, 0] - down * spectrum[part, 1]

    def edge(d):
        there = lax.rem(gz + d, NGZ)
        side = jnp.where(there > gz, 0, 1)
        return pltpu.make_async_remote_copy(
            src_ref=edges.at[side],
            dst_ref=edge_in.at[gz],
            send_sem=edge_send.at[d],
            recv_sem=edge_recv.at[d],
            device_id=(there, gy),
            device_id_type=MESH,
        )

    for d in range(1, NGZ):
        edge(d).start()
    edge_in[gz] = jnp.zeros((2, CAP, NY), F32)

    first_pivot, last_pivot = pivots[0, low_level], pivots[1, high_level]
    cross_up, cross_down = below[high_level], above[low_level]
    inverse = 1.0 / (first_pivot * last_pivot - cross_up * cross_down)
    beneath = jnp.maximum(low_level - 1, 0)
    over = jnp.minimum(high_level + 1, NZ - 1)
    from_below = below[low_level] * pivots[2, beneath]
    from_above = above[high_level] * pivots[3, over]
    for d in range(1, NGZ):
        edge(d).wait()
    for part in range(2):
        reached = jnp.zeros((CAP, NY), F32)
        for block in range(NGZ - 1):
            new = edge_in[block, part]
            if block > 0:
                k = DEPTH * block
                new = new + (below[k] * below[k + 1]) * pivots[2, k - 1] * pivots[2, k] * reached
            reached = jnp.where(block < gz, new, reached)
        lower = spectrum[part, 0] - from_below * reached
        reached = jnp.zeros((CAP, NY), F32)
        for block in range(NGZ - 1, 0, -1):
            new = edge_in[block, part]
            if block < NGZ - 1:
                k = DEPTH * block
                new = new + (above[k] * above[k + 1]) * pivots[3, k + 1] * pivots[3, k + 2] * reached
            reached = jnp.where(block > gz, new, reached)
        upper = spectrum[part, 1] - from_above * reached
        out[part, 0] = (last_pivot * lower - cross_down * upper) * inverse
        out[part, 1] = (first_pivot * upper - cross_up * lower) * inverse


def per_device(velocity_x, velocity_y, velocity_z, owners, below, above, metric):
    anywhere = pl.BlockSpec(memory_space=pl.ANY)
    scalars = pl.BlockSpec(memory_space=pltpu.SMEM)
    consts = [jnp.asarray(t) for t in tables()]
    dma = pltpu.SemaphoreType.DMA
    result = pl.pallas_call(
        kernel,
        out_shape=jax.ShapeDtypeStruct((2, DEPTH, CAP, NY), F32),
        in_specs=[anywhere] * 3 + [pl.BlockSpec(memory_space=pltpu.VMEM)] + [scalars] * 3 + [anywhere] * 5,
        out_specs=pl.BlockSpec(memory_space=pltpu.VMEM),
        scratch_shapes=[
            pltpu.VMEM((3, DEPTH, ROWS, NX), BF16),
            pltpu.VMEM((3 * DEPTH * ROWS * 16, 128), F32),
            pltpu.VMEM((3, 6, 20, 16, 128), BF16),
            pltpu.VMEM((6, 4, 18, 16, 128), F32),
            pltpu.VMEM((2, 256, 256), BF16),
            pltpu.VMEM((NGY, 8, 128), F32),
            pltpu.VMEM((NGY, 8, 128), F32),
        ]
        + [pltpu.VMEM(c.shape, c.dtype) for c in consts]
        + [
            pltpu.VMEM((2, 512, KXR), BF16),
            pltpu.VMEM((4, NZ, CAP, NY), F32),
            pltpu.VMEM((2, 2, CAP, NY), F32),
            pltpu.VMEM((NGZ, 2, CAP, NY), F32),
            pltpu.VMEM((2, DEPTH, CAP, NY), F32),
            dma((8,)), dma((10,)), dma((10,)), dma((NGY,)), dma((NGY,)), dma((NGZ,)), dma((NGZ,)),
            dma(()),
        ],
        compiler_params=pltpu.CompilerParams(collective_id=0, has_side_effects=True),
    )(velocity_x, velocity_y, velocity_z, owners.reshape(1, KXR), below, above, metric, *consts)
    return jnp.transpose(result, (2, 0, 1, 3))[None]


def solution(mesh):
    placed = (P("gz", "gy", None), P("gz", "gy", None), P("gz", "gy", None), P(), P(), P(), P())
    return jax.shard_map(
        per_device,
        mesh=mesh,
        in_specs=placed,
        out_specs=P("gy", None, None, "gz", None),
        check_vma=False,
    )
```

time: 253 us -> 52.3 us (0.21)
  the two profiles are of different devices: /device:TPU:8 before, /device:TPU:1 now
where the time goes in v1:
time: 52.3 us; the launch traced here: 52.2 us
  Pallas kernels  50.3 us (96%)
  local copies, waits for them, and re-layouts  1.86 us (4%)
    pallas_call x1, Pallas kernels, per_device(): pl.pallas_call(kernel, out_shape=jax.ShapeDtypeStruct((2, DEPTH, CAP, NY)...  50.3 us
    broadcast_in_dim x1, local copies, waits for them, and re-layouts, per_device(): return jnp.transpose(result, (2, 0, 1, 3))[None]  1.86 us

profile of v1, /device:TPU:1, one launch (start us, length us, event | category | flops | bytes accessed | tf_op | source)
XLA Modules:
  0.0 52.2 jit_solution(828886173442441947)
XLA Ops:
  0.0 50.3 %shard_map.118 = f32[2,2,16,1024]{3,2,1,0:T(8,128)} custom-call(bf16[2,16,2048]{2,1,0:T(8,128)(2,1)} %vx.1, bf16[2,16,2048]{2,1,0:T(8,128)(2,1)} %vy.1, bf16[2,16,2048]{2,1,0:T(8,128)(2,1)} %vz.1, s32[1,512]{1,0:T(1,128)} %bitcast.5, f32[8]{0:T(128)} %below.1, f32[8]{0:T(128)} %above.1, f32[8]{0:T(128)} %metric.1, ...), custom_call_target="tpu_custom_call" | custom-call | tf_op jit(solution)/shard_map/pallas_call | solution.py:452
  50.3 1.9 %copy.13 = f32[1,16,2,2,1024]{4,3,2,1,0:T(2,128)} copy(f32[1,16,2,2,1024]{4,1,3,2,0:T(8,128)} %bitcast.4) | data formatting | bytes 524288 | tf_op jit(solution)/shard_map/broadcast_in_dim | solution.py:478

commit v2 on v1

--- a/solution.py
+++ b/solution.py
@@ -19,6 +19,7 @@
 NX, NY, NZ, KXR, CAP = 2048, 1024, 8, 512, 16
 NGZ, NGY = 4, 64
 DEPTH, ROWS = 2, 16
+STRAIGHT = ((1, 0), (-1, 0), (0, 1), (0, -1))
 DIAGONAL = ((1, 1), (1, -1), (-1, 1), (-1, -1))
 
 
@@ -105,9 +106,9 @@
 def kernel(
     vx, vy, vz, owners, below, above, metric, x_first_in, x_second_in, y_first_in, turn_in,
     y_second_in, out,
-    own, spread, ext, stress, source, outgoing, received, x_first, x_second, y_first, turn,
+    own, spread, ext, stress, flat, begun, source, outgoing, received, x_first, x_second, y_first, turn,
     y_second, chosen, pivots, edges, edge_in, spectrum,
-    in_sem, halo_send, halo_recv, all_send, all_recv, edge_send, edge_recv, own_sem,
+    in_sem, halo_send, halo_recv, all_send, all_recv, edge_send, edge_recv, own_sem, meeting,
 ):
     gz, gy = lax.axis_index("gz"), lax.axis_index("gy")
 
@@ -125,13 +126,7 @@
 
     barrier = pltpu.get_barrier_semaphore()
 
-    @pl.loop(1, NGY)
-    def _(d):
-        pl.semaphore_signal(barrier, inc=1, device_id=peer(0, d), device_id_type=MESH)
-
-    for d in range(1, NGZ):
-        pl.semaphore_signal(barrier, inc=1, device_id=peer(d, 0), device_id_type=MESH)
-    for dz, dy in DIAGONAL:
+    for dz, dy in STRAIGHT + DIAGONAL:
         pl.semaphore_signal(barrier, inc=1, device_id=peer(dz, dy), device_id_type=MESH)
 
     for c in range(3):
@@ -145,34 +140,51 @@
                 ].astype(F32)
             ext[c, z + 2, 2:18] = spread[base : base + 256, :].reshape(16, 16, 128).astype(BF16)
 
-    pl.semaphore_wait(barrier, NGY - 1 + NGZ - 1 + len(DIAGONAL))
-
-    def level_span(dz):
-        return pl.ds({1: 0, 0: 2, -1: 4}[dz], 2)
-
-    def halo(index, dz, dy, levels_from, levels_to):
-        rows_from = pl.ds({1: 16, 0: 2, -1: 2}[dy], 16 if dy == 0 else 2)
-        rows_to = pl.ds({1: 0, 0: 2, -1: 18}[dy], 16 if dy == 0 else 2)
+    pl.semaphore_wait(barrier, len(STRAIGHT) + len(DIAGONAL))
+
+    def copy_to(index, dz, dy, given, kept):
         return pltpu.make_async_remote_copy(
-            src_ref=ext.at[:, levels_from, rows_from],
-            dst_ref=ext.at[:, levels_to, rows_to],
+            src_ref=ext.at[:, given[0], given[1]],
+            dst_ref=ext.at[:, kept[0], kept[1]],
             send_sem=halo_send.at[index],
             recv_sem=halo_recv.at[index],
             device_id=peer(dz, dy),
             device_id_type=MESH,
         )
 
+    def rows(start, count):
+        return pl.ds(start, count)
+
     near = [
-        halo(0, 1, 0, pl.ds(3, 1), pl.ds(1, 1)),
-        halo(1, -1, 0, pl.ds(2, 1), pl.ds(4, 1)),
-        halo(2, 0, 1, level_span(0), level_span(0)),
-        halo(3, 0, -1, level_span(0), level_span(0)),
+        copy_to(0, 1, 0, (pl.ds(3, 1), rows(2, 16)), (pl.ds(1, 1), rows(2, 16))),
+        copy_to(1, -1, 0, (pl.ds(2, 1), rows(2, 16)), (pl.ds(4, 1), rows(2, 16))),
     ]
-    for index, (dz, dy) in enumerate(DIAGONAL):
-        near.append(halo(4 + index, dz, dy, level_span(0), level_span(dz)))
-    far = [halo(8, 1, 0, pl.ds(2, 1), pl.ds(0, 1)), halo(9, -1, 0, pl.ds(3, 1), pl.ds(5, 1))]
-    for copy in near + far:
+    rims = [
+        copy_to(2, 0, 1, (pl.ds(2, 2), rows(16, 2)), (pl.ds(2, 2), rows(0, 2))),
+        copy_to(3, 0, -1, (pl.ds(2, 2), rows(2, 2)), (pl.ds(2, 2), rows(18, 2))),
+    ]
+    far = [
+        copy_to(4, 1, 1, (pl.ds(2, 1), rows(17, 1)), (pl.ds(0, 1), rows(1, 1))),
+        copy_to(5, 1, -1, (pl.ds(2, 1), rows(2, 1)), (pl.ds(0, 1), rows(18, 1))),
+        copy_to(6, -1, 1, (pl.ds(3, 1), rows(17, 1)), (pl.ds(5, 1), rows(1, 1))),
+        copy_to(7, -1, -1, (pl.ds(3, 1), rows(2, 1)), (pl.ds(5, 1), rows(18, 1))),
+        copy_to(8, 1, 0, (pl.ds(2, 1), rows(2, 16)), (pl.ds(0, 1), rows(2, 16))),
+        copy_to(9, -1, 0, (pl.ds(3, 1), rows(2, 16)), (pl.ds(5, 1), rows(2, 16))),
+    ]
+    corners = [
+        copy_to(10, 0, 1, (pl.ds(1, 1), rows(16, 2)), (pl.ds(1, 1), rows(0, 2))),
+        copy_to(11, 0, 1, (pl.ds(4, 1), rows(16, 2)), (pl.ds(4, 1), rows(0, 2))),
+        copy_to(12, 0, -1, (pl.ds(1, 1), rows(2, 2)), (pl.ds(1, 1), rows(18, 2))),
+        copy_to(13, 0, -1, (pl.ds(4, 1), rows(2, 2)), (pl.ds(4, 1), rows(18, 2))),
+    ]
+    for copy in near + rims + far:
         copy.start()
+
+    def meet(number, peers):
+        for dz, dy in peers:
+            pl.semaphore_signal(meeting.at[number], inc=1, device_id=peer(dz, dy), device_id_type=MESH)
+
+    meet(0, STRAIGHT)
 
     owner_row = owners[...]
     kx_row = mode_of(iota((1, KXR), 1))
@@ -195,6 +207,9 @@
     radius = own_kx * own_kx + ky * ky
     inside = jnp.where(radius <= float(KXR * KXR), 1.0, 0.0) * own_ok
 
+    pl.semaphore_wait(meeting.at[0], len(STRAIGHT))
+    meet(1, ((0, 2), (0, -2)))
+
     shift = BASE_SHIFT + MODE_SHIFT * (radius / float(KXR * KXR))
     for k in range(NZ):
         pivot = -(below[k] + above[k] + metric[k] * shift)
@@ -209,6 +224,9 @@
         pivots[1, k] = pivot
         pivots[3, k] = 1.0 / pivot
 
+    pl.semaphore_wait(meeting.at[1], 2)
+    meet(2, ((0, 4), (0, -4)))
+
     def zero_rim(levels):
         @pl.when(gy == 0)
         def _():
@@ -220,23 +238,43 @@
             for level in levels:
                 ext[:, level, 18:20] = jnp.zeros((3, 2, 16, 128), BF16)
 
-    def zero_level(edge, level):
+    def zero_level(edge, level, start, count):
         @pl.when(gz == edge)
         def _():
             for c in range(3):
-                ext[c, level] = jnp.zeros((20, 16, 128), BF16)
+                ext[c, level, start : start + count] = jnp.zeros((count, 16, 128), BF16)
 
     def at(c, level, row, count):
         return ext[c, level, pl.ds(row, count)].astype(F32)
 
-    def stress_rows(level, wanted, row, count):
+    def flat_slopes(level, row, count):
         centre = [at(c, level, row, count) for c in range(3)]
-        grad = []
-        for c in range(3):
-            dx = (next_x(centre[c], True) - next_x(centre[c], False)) * 0.5
-            dy = (at(c, level, row + 1, count) - at(c, level, row - 1, count)) * 0.5
-            dz = (at(c, level + 1, row, count) - at(c, level - 1, row, count)) * 0.5
-            grad.append((dx, dy, dz))
+        dx = [(next_x(f, True) - next_x(f, False)) * 0.5 for f in centre]
+        dy = [(at(c, level, row + 1, count) - at(c, level, row - 1, count)) * 0.5 for c in range(3)]
+        return dx, dy
+
+    def slopes_z(level, row, count):
+        return [(at(c, level + 1, row, count) - at(c, level - 1, row, count)) * 0.5 for c in range(3)]
+
+    for copy in near:
+        copy.wait_recv()
+    zero_level(0, 1, 2, 16)
+    zero_level(NGZ - 1, 4, 2, 16)
+    for copy in corners:
+        copy.start()
+    for copy in rims + corners:
+        copy.wait_recv()
+    for copy in corners:
+        copy.wait_send()
+    zero_level(0, 1, 0, 20)
+    zero_level(NGZ - 1, 4, 0, 20)
+    zero_rim((1, 2, 3, 4))
+
+    @pl.loop(0, 18, unroll=3)
+    def _(step):
+        level, row, count = 2 + step // 9, 1 + 2 * lax.rem(step, 9), 2
+        dx, dy = flat_slopes(level, row, count)
+        grad = list(zip(dx, dy, slopes_z(level, row, count)))
         strain = {
             (i, j): grad[i][i] if i == j else 0.5 * (grad[i][j] + grad[j][i])
             for i in range(3) for j in range(i, 3)
@@ -247,52 +285,78 @@
         )
         viscous = 2.0 * SMAG_COEF * jnp.sqrt(squared + STRAIN_FLOOR)
         for index, pair in enumerate(((2, 2), (0, 2), (1, 2), (0, 0), (0, 1), (1, 1))):
-            if index < wanted:
-                stress[index, level - 1, pl.ds(row - 1, count)] = viscous * strain[pair]
-
-    for copy in near:
-        copy.wait_recv()
-    zero_level(0, 1)
-    zero_level(NGZ - 1, 4)
-    zero_rim((1, 2, 3, 4))
-
-    @pl.loop(0, 18)
+            stress[index, level - 1, pl.ds(row - 1, count)] = viscous * strain[pair]
+
+    pl.semaphore_wait(meeting.at[2], 2)
+    meet(3, ((0, 8), (0, -8)))
+
+    @pl.loop(0, 18, unroll=3)
     def _(step):
-        stress_rows(2 + step // 9, 6, 1 + 2 * lax.rem(step, 9), 2)
+        side, row, count = step // 9, 1 + 2 * lax.rem(step, 9), 2
+        dx, dy = flat_slopes(1 + 3 * side, row, count)
+        mixed = 0.5 * (dy[0] + dx[1])
+        squared = 2.0 * (dx[0] * dx[0] + dy[1] * dy[1]) + 4.0 * mixed * mixed + STRAIN_FLOOR
+        for index, value in enumerate((squared, dx[2], dy[2])):
+            flat[index, side, pl.ds(row - 1, count)] = value
+
+    for z in range(DEPTH):
+
+        @pl.loop(0, 8, unroll=4)
+        def _(step):
+            row = 2 * step
+            sign = 1.0 if z == 0 else -1.0
+
+            def part(index, dz, dy):
+                return stress[index, z + 1 + dz, pl.ds(row + 1 + dy, 2)]
+
+            def wind(c, dz, dy):
+                return at(c, z + 2 + dz, row + 2 + dy, 2)
+
+            beside = 1 - 2 * z
+            total = 0.5 * (wind(1, 0, 1) - wind(1, 0, -1) + wind(2, 1, 0) - wind(2, -1, 0))
+            total = total + part(5, 0, 1) + part(5, 0, -1) + part(0, beside, 0)
+            total = total - 2.0 * (part(3, 0, 0) + part(5, 0, 0) + part(0, 0, 0))
+            total = total + (0.5 * sign) * (part(2, beside, 1) - part(2, beside, -1))
+            odd = 0.5 * (wind(0, 0, 0) + part(4, 0, 1) - part(4, 0, -1) + sign * part(1, beside, 0))
+            even = part(3, 0, 0)
+            total = total + next_x(even + odd, True) + next_x(even - odd, False)
+            begun[z, pl.ds(row, 2)] = total
+
+    pl.semaphore_wait(meeting.at[3], 2)
+    meet(4, ((0, 16), (0, -16)))
 
     for copy in far:
         copy.wait_recv()
-    zero_level(0, 0)
-    zero_level(NGZ - 1, 5)
+    zero_level(0, 0, 0, 20)
+    zero_level(NGZ - 1, 5, 0, 20)
     zero_rim((0, 5))
 
-    @pl.loop(0, 18)
+    @pl.loop(0, 18, unroll=3)
     def _(step):
-        stress_rows(1 + 3 * (step // 9), 3, 1 + 2 * lax.rem(step, 9), 2)
+        side, row, count = step // 9, 1 + 2 * lax.rem(step, 9), 2
+        level = 1 + 3 * side
+        dz = slopes_z(level, row, count)
+        squared, dx_w, dy_w = (flat[index, side, pl.ds(row - 1, count)] for index in range(3))
+        strain_x, strain_y = 0.5 * (dz[0] + dx_w), 0.5 * (dz[1] + dy_w)
+        squared = squared + 2.0 * dz[2] * dz[2] + 4.0 * (strain_x * strain_x + strain_y * strain_y)
+        viscous = 2.0 * SMAG_COEF * jnp.sqrt(squared)
+        for index, value in enumerate((dz[2], strain_x, strain_y)):
+            stress[index, level - 1, pl.ds(row - 1, count)] = viscous * value
 
     for z in range(DEPTH):
 
-        @pl.loop(0, 8)
+        @pl.loop(0, 8, unroll=4)
         def _(step):
             row = 2 * step
-
-            def part(index, dz, dy):
-                return stress[index, z + 1 + dz, pl.ds(row + 1 + dy, 2)]
-
-            def wind(c, dz, dy):
-                return at(c, z + 2 + dz, row + 2 + dy, 2)
-
-            total = 0.5 * (wind(1, 0, 1) - wind(1, 0, -1) + wind(2, 1, 0) - wind(2, -1, 0))
-            total = total + part(5, 0, 1) + part(5, 0, -1) + part(0, 1, 0) + part(0, -1, 0)
-            total = total - 2.0 * (part(3, 0, 0) + part(5, 0, 0) + part(0, 0, 0))
-            total = total + 0.5 * (
-                part(2, 1, 1) - part(2, 1, -1) - part(2, -1, 1) + part(2, -1, -1)
-            )
-            odd = 0.5 * (
-                wind(0, 0, 0) + part(4, 0, 1) - part(4, 0, -1) + part(1, 1, 0) - part(1, -1, 0)
-            )
-            even = part(3, 0, 0)
-            total = total + next_x(even + odd, True) + next_x(even - odd, False)
+            sign = -1.0 if z == 0 else 1.0
+
+            def part(index, dy):
+                return stress[index, 3 * z, pl.ds(row + 1 + dy, 2)]
+
+            odd = (0.5 * sign) * part(1, 0)
+            total = begun[z, pl.ds(row, 2)] + part(0, 0)
+            total = total + (0.5 * sign) * (part(2, 1) - part(2, -1))
+            total = total + next_x(odd, True) - next_x(odd, False)
             high, low = split(total.reshape(32, 128))
             start = pl.multiple_of(32 * step, 32)
             source[0, pl.ds(start, 32), z * 128 : (z + 1) * 128] = high
@@ -304,10 +368,12 @@
     first = dot(x_first[0], high) + dot(x_first[0], low) + dot(x_first[1], high)
     parts = []
     for i in range(8):
-        rows = first[32 * i : 32 * i + 32]
+        lines = first[32 * i : 32 * i + 32]
         left = jnp.concatenate(
             [
-                jnp.concatenate([rows[0:16, 128 * z : 128 * z + 128], rows[16:32, 128 * z : 128 * z + 128]], 1)
+                jnp.concatenate(
+                    [lines[0:16, 128 * z : 128 * z + 128], lines[16:32, 128 * z : 128 * z + 128]], 1
+                )
                 for z in range(DEPTH)
             ],
             0,
@@ -335,6 +401,8 @@
     together = jnp.where(iota((512, 128), 1) < 64, slots[0], slots[1])
     outgoing[...] = together.reshape(NGY, 8, 128)
 
+    pl.semaphore_wait(meeting.at[4], 2)
+
     def exchange(d):
         there = lax.rem(gy + d, NGY)
         return pltpu.make_async_remote_copy(
@@ -352,7 +420,7 @@
 
     keep = pltpu.make_async_copy(outgoing.at[gy], received.at[gy], own_sem)
     keep.start()
-    for copy in near + far:
+    for copy in near + rims + far:
         copy.wait_send()
     keep.wait()
 
@@ -360,14 +428,14 @@
     def _(d):
         exchange(d).wait()
 
-    rows = []
-    flat = received.reshape(NGY * 8, 128)
+    pieces = []
+    arrived = received.reshape(NGY * 8, 128)
     for clo in range(8):
-        turned = flat[pl.ds(clo, NGY, stride=8), :].T
+        turned = arrived[pl.ds(clo, NGY, stride=8), :].T
         for chi in range(2):
             real, imag = turned[64 * chi : 64 * chi + 32], turned[64 * chi + 32 : 64 * chi + 64]
-            rows.append(jnp.concatenate([real, imag], 1))
-    left = jnp.concatenate(rows, 0)
+            pieces.append(jnp.concatenate([real, imag], 1))
+    left = jnp.concatenate(pieces, 0)
     high, low = split(left)
     both = dot(jnp.concatenate([high, low], 0), y_first[...])
     value = both[0:512, 0:128] + both[512:1024, 0:128] + both[0:512, 128:256]
@@ -440,8 +508,14 @@
                 new = new + (above[k] * above[k + 1]) * pivots[3, k + 1] * pivots[3, k + 2] * reached
             reached = jnp.where(block > gz, new, reached)
         upper = spectrum[part, 1] - from_above * reached
-        out[part, 0] = (last_pivot * lower - cross_down * upper) * inverse
-        out[part, 1] = (first_pivot * upper - cross_up * lower) * inverse
+        for z, value in enumerate(
+            (last_pivot * lower - cross_down * upper, first_pivot * upper - cross_up * lower)
+        ):
+            value = value * inverse
+            for tile in range(NY // 128):
+                out[pl.ds(part * 16 + tile * 2 + z, CAP, stride=32), :] = value[
+                    :, tile * 128 : (tile + 1) * 128
+                ]
 
 
 def per_device(velocity_x, velocity_y, velocity_z, owners, below, above, metric):
@@ -451,7 +525,7 @@
     dma = pltpu.SemaphoreType.DMA
     result = pl.pallas_call(
         kernel,
-        out_shape=jax.ShapeDtypeStruct((2, DEPTH, CAP, NY), F32),
+        out_shape=jax.ShapeDtypeStruct((2 * DEPTH * CAP * NY // 128, 128), F32),
         in_specs=[anywhere] * 3 + [pl.BlockSpec(memory_space=pltpu.VMEM)] + [scalars] * 3 + [anywhere] * 5,
         out_specs=pl.BlockSpec(memory_space=pltpu.VMEM),
         scratch_shapes=[
@@ -459,6 +533,8 @@
             pltpu.VMEM((3 * DEPTH * ROWS * 16, 128), F32),
             pltpu.VMEM((3, 6, 20, 16, 128), BF16),
             pltpu.VMEM((6, 4, 18, 16, 128), F32),
+            pltpu.VMEM((3, 2, 18, 16, 128), F32),
+            pltpu.VMEM((DEPTH, ROWS, 16, 128), F32),
             pltpu.VMEM((2, 256, 256), BF16),
             pltpu.VMEM((NGY, 8, 128), F32),
             pltpu.VMEM((NGY, 8, 128), F32),
@@ -470,12 +546,14 @@
             pltpu.VMEM((2, 2, CAP, NY), F32),
             pltpu.VMEM((NGZ, 2, CAP, NY), F32),
             pltpu.VMEM((2, DEPTH, CAP, NY), F32),
-            dma((8,)), dma((10,)), dma((10,)), dma((NGY,)), dma((NGY,)), dma((NGZ,)), dma((NGZ,)),
+            dma((8,)), dma((14,)), dma((14,)), dma((NGY,)), dma((NGY,)), dma((NGZ,)), dma((NGZ,)),
             dma(()),
+            pltpu.SemaphoreType.REGULAR((5,)),
         ],
         compiler_params=pltpu.CompilerParams(collective_id=0, has_side_effects=True),
     )(velocity_x, velocity_y, velocity_z, owners.reshape(1, KXR), below, above, metric, *consts)
-    return jnp.transpose(result, (2, 0, 1, 3))[None]
+    result = result.reshape(CAP, 2, NY // 128, DEPTH, 128)
+    return jnp.transpose(result, (0, 1, 3, 2, 4)).reshape(1, CAP, 2, DEPTH, NY)
 
 
 def solution(mesh):

time: 52.3 us -> 48.3 us (0.924)
  Pallas kernels: 50.3 us -> 46.5 us
    pallas_call x1, Pallas kernels: 50.3 us -> 46.5 us  [per_device(): pl.pallas_call(kernel, out_shape=jax.ShapeDtypeStruct((2 * DEPTH * CAP *...]
    broadcast_in_dim x1 -> x0, local copies, waits for them, and re-layouts: 1.86 us -> none  [per_device(): return jnp.transpose(result, (2, 0, 1, 3))[None]]
    unnamed x0 -> x1, local copies, waits for them, and re-layouts: none -> 1.67 us
where the time goes in v2:
time: 48.3 us; the launch traced here: 48.2 us
  Pallas kernels  46.5 us (96%)
  local copies, waits for them, and re-layouts  1.67 us (3%)
    pallas_call x1, Pallas kernels, per_device(): pl.pallas_call(kernel, out_shape=jax.ShapeDtypeStruct((2 * DEPTH * CAP *...  46.5 us
    unnamed x1, local copies, waits for them, and re-layouts  1.67 us

profile of v2, /device:TPU:1, one launch (start us, length us, event | category | flops | bytes accessed | tf_op | source)
XLA Modules:
  0.0 48.2 jit_solution(2608208221885487450)
XLA Ops:
  0.0 46.5 %shard_map.118 = f32[512,128]{1,0:T(8,128)} custom-call(bf16[2,16,2048]{2,1,0:T(8,128)(2,1)} %vx.1, bf16[2,16,2048]{2,1,0:T(8,128)(2,1)} %vy.1, bf16[2,16,2048]{2,1,0:T(8,128)(2,1)} %vz.1, s32[1,512]{1,0:T(1,128)} %bitcast.7, f32[8]{0:T(128)} %below.1, f32[8]{0:T(128)} %above.1, f32[8]{0:T(128)} %metric.1, bf16[2,256,256]{2,1,0:T(8,128)(2,1)} %constant.10.clone.x_first_in, ...), custom_call_target="tpu_custom_call" | custom-call | tf_op jit(solution)/shard_map/pallas_call | solution.py:526
  46.5 1.7 %copy.15 = f32[1,16,2,2,1024]{4,3,2,1,0:T(2,128)} copy(f32[1,16,2,2,1024]{4,3,2,1,0:T(2,128)} %bitcast.6) | data formatting | bytes 524288

commit v3 on v2

--- a/solution.py
+++ b/solution.py
@@ -107,7 +107,7 @@
     vx, vy, vz, owners, below, above, metric, x_first_in, x_second_in, y_first_in, turn_in,
     y_second_in, out,
     own, spread, ext, stress, flat, begun, source, outgoing, received, x_first, x_second, y_first, turn,
-    y_second, chosen, pivots, edges, edge_in, spectrum,
+    y_second, chosen, pivots, edges, edge_in, steps, steps_in, spectrum,
     in_sem, halo_send, halo_recv, all_send, all_recv, edge_send, edge_recv, own_sem, meeting,
 ):
     gz, gy = lax.axis_index("gz"), lax.axis_index("gy")
@@ -403,20 +403,20 @@
 
     pl.semaphore_wait(meeting.at[4], 2)
 
-    def exchange(d):
-        there = lax.rem(gy + d, NGY)
+    def exchange(given, kept, there):
         return pltpu.make_async_remote_copy(
-            src_ref=outgoing.at[there],
-            dst_ref=received.at[gy],
-            send_sem=all_send.at[d],
-            recv_sem=all_recv.at[d],
+            src_ref=given,
+            dst_ref=kept,
+            send_sem=all_send,
+            recv_sem=all_recv,
             device_id=(gz, there),
             device_id_type=MESH,
         )
 
-    @pl.loop(1, NGY)
-    def _(d):
-        exchange(d).start()
+    @pl.loop(0, NGY - 1, unroll=3)
+    def _(k):
+        there = lax.rem(gy + NGY // 2 + (k + 1) // 2 * (1 - 2 * lax.rem(k, 2)) + NGY, NGY)
+        exchange(outgoing.at[there], received.at[gy], there).start()
 
     keep = pltpu.make_async_copy(outgoing.at[gy], received.at[gy], own_sem)
     keep.start()
@@ -424,9 +424,8 @@
         copy.wait_send()
     keep.wait()
 
-    @pl.loop(1, NGY)
-    def _(d):
-        exchange(d).wait()
+    others = pl.ds(0, NGY - 1)
+    exchange(outgoing.at[others], received.at[others], gy).wait()
 
     pieces = []
     arrived = received.reshape(NGY * 8, 128)
@@ -462,25 +461,38 @@
     low_level, high_level = DEPTH * gz, DEPTH * gz + 1
     up = below[high_level] * pivots[2, low_level]
     down = above[low_level] * pivots[3, high_level]
-    for part in range(2):
-        edges[0, part] = spectrum[part, 1] - up * spectrum[part, 0]
-        edges[1, part] = spectrum[part, 0] - down * spectrum[part, 1]
-
-    def edge(d):
+    for side in range(2):
+        if side == 0:
+            values = [spectrum[part, 1] - up * spectrum[part, 0] for part in range(2)]
+        else:
+            values = [spectrum[part, 0] - down * spectrum[part, 1] for part in range(2)]
+        largest = jnp.maximum(jnp.abs(values[0]), jnp.abs(values[1]))
+        largest = jnp.maximum(jnp.max(largest, axis=1, keepdims=True), 1e-30)
+        scale = 32767.0 / largest
+        for part in range(2):
+            edges[side, part] = jnp.floor(values[part] * scale + 0.5).astype(I32).astype(jnp.int16)
+        steps[side] = jnp.broadcast_to(largest * (1.0 / 32767.0), (CAP, 128))
+
+    def edge(d, given, kept, kind):
         there = lax.rem(gz + d, NGZ)
-        side = jnp.where(there > gz, 0, 1)
         return pltpu.make_async_remote_copy(
-            src_ref=edges.at[side],
-            dst_ref=edge_in.at[gz],
-            send_sem=edge_send.at[d],
-            recv_sem=edge_recv.at[d],
+            src_ref=given.at[jnp.where(there > gz, 0, 1)],
+            dst_ref=kept.at[gz],
+            send_sem=edge_send.at[kind, d],
+            recv_sem=edge_recv.at[kind, d],
             device_id=(there, gy),
             device_id_type=MESH,
         )
 
-    for d in range(1, NGZ):
-        edge(d).start()
-    edge_in[gz] = jnp.zeros((2, CAP, NY), F32)
+    crossing = [
+        edge(d, given, kept, kind)
+        for d in (2, 1, 3)
+        for kind, (given, kept) in enumerate(((edges, edge_in), (steps, steps_in)))
+    ]
+    for copy in crossing:
+        copy.start()
+    edge_in[gz] = jnp.zeros((2, CAP, NY), jnp.int16)
+    steps_in[gz] = jnp.zeros((CAP, 128), F32)
 
     first_pivot, last_pivot = pivots[0, low_level], pivots[1, high_level]
     cross_up, cross_down = below[high_level], above[low_level]
@@ -489,12 +501,17 @@
     over = jnp.minimum(high_level + 1, NZ - 1)
     from_below = below[low_level] * pivots[2, beneath]
     from_above = above[high_level] * pivots[3, over]
-    for d in range(1, NGZ):
-        edge(d).wait()
+    for copy in crossing:
+        copy.wait()
+
+    def edge_of(block, part):
+        step = jnp.concatenate([steps_in[block]] * (NY // 128), 1)
+        return edge_in[block, part].astype(I32).astype(F32) * step
+
     for part in range(2):
         reached = jnp.zeros((CAP, NY), F32)
         for block in range(NGZ - 1):
-            new = edge_in[block, part]
+            new = edge_of(block, part)
             if block > 0:
                 k = DEPTH * block
                 new = new + (below[k] * below[k + 1]) * pivots[2, k - 1] * pivots[2, k] * reached
@@ -502,7 +519,7 @@
         lower = spectrum[part, 0] - from_below * reached
         reached = jnp.zeros((CAP, NY), F32)
         for block in range(NGZ - 1, 0, -1):
-            new = edge_in[block, part]
+            new = edge_of(block, part)
             if block < NGZ - 1:
                 k = DEPTH * block
                 new = new + (above[k] * above[k + 1]) * pivots[3, k + 1] * pivots[3, k + 2] * reached
@@ -525,7 +542,7 @@
     dma = pltpu.SemaphoreType.DMA
     result = pl.pallas_call(
         kernel,
-        out_shape=jax.ShapeDtypeStruct((2 * DEPTH * CAP * NY // 128, 128), F32),
+        out_shape=pltpu.VMEM((2 * DEPTH * CAP * NY // 128, 128), F32),
         in_specs=[anywhere] * 3 + [pl.BlockSpec(memory_space=pltpu.VMEM)] + [scalars] * 3 + [anywhere] * 5,
         out_specs=pl.BlockSpec(memory_space=pltpu.VMEM),
         scratch_shapes=[
@@ -543,10 +560,12 @@
         + [
             pltpu.VMEM((2, 512, KXR), BF16),
             pltpu.VMEM((4, NZ, CAP, NY), F32),
-            pltpu.VMEM((2, 2, CAP, NY), F32),
-            pltpu.VMEM((NGZ, 2, CAP, NY), F32),
+            pltpu.VMEM((2, 2, CAP, NY), jnp.int16),
+            pltpu.VMEM((NGZ, 2, CAP, NY), jnp.int16),
+            pltpu.VMEM((2, CAP, 128), F32),
+            pltpu.VMEM((NGZ, CAP, 128), F32),
             pltpu.VMEM((2, DEPTH, CAP, NY), F32),
-            dma((8,)), dma((14,)), dma((14,)), dma((NGY,)), dma((NGY,)), dma((NGZ,)), dma((NGZ,)),
+            dma((8,)), dma((14,)), dma((14,)), dma(()), dma(()), dma((2, NGZ)), dma((2, NGZ)),
             dma(()),
             pltpu.SemaphoreType.REGULAR((5,)),
         ],

time: 48.3 us -> 42.5 us (0.88)
  Pallas kernels: 46.5 us -> 41.7 us
  local copies, waits for them, and re-layouts: 1.67 us -> 0.71 us
    pallas_call x1, Pallas kernels: 46.5 us -> 41.7 us  [per_device(): pl.pallas_call(kernel, out_shape=pltpu.VMEM((2 * DEPTH * CAP * NY // 128,...]
    unnamed x1, local copies, waits for them, and re-layouts: 1.67 us -> 0.71 us
where the time goes in v3:
time: 42.5 us; the launch traced here: 42.4 us
  Pallas kernels  41.7 us (98%)
  local copies, waits for them, and re-layouts  0.71 us (2%)
    pallas_call x1, Pallas kernels, per_device(): pl.pallas_call(kernel, out_shape=pltpu.VMEM((2 * DEPTH * CAP * NY // 128,...  41.7 us

profile of v3, /device:TPU:1, one launch (start us, length us, event | category | flops | bytes accessed | tf_op | source)
XLA Modules:
  0.0 42.4 jit_solution(11627711419911712899)
XLA Ops:
  0.0 41.7 %shard_map.118 = f32[512,128]{1,0:T(8,128)S(1)} custom-call(bf16[2,16,2048]{2,1,0:T(8,128)(2,1)} %vx.1, bf16[2,16,2048]{2,1,0:T(8,128)(2,1)} %vy.1, bf16[2,16,2048]{2,1,0:T(8,128)(2,1)} %vz.1, s32[1,512]{1,0:T(1,128)} %bitcast.7, f32[8]{0:T(128)} %below.1, f32[8]{0:T(128)} %above.1, f32[8]{0:T(128)} %metric.1, ...), custom_call_target="tpu_custom_call" | custom-call | tf_op jit(solution)/shard_map/pallas_call | solution.py:543
  41.7 0.7 %copy.15 = f32[1,16,2,2,1024]{4,3,2,1,0:T(2,128)} copy(f32[1,16,2,2,1024]{4,3,2,1,0:T(2,128)S(1)} %bitcast.6) | data formatting | bytes 524288

commit v4 on v3

--- a/solution.py
+++ b/solution.py
@@ -20,7 +20,6 @@
 NGZ, NGY = 4, 64
 DEPTH, ROWS = 2, 16
 STRAIGHT = ((1, 0), (-1, 0), (0, 1), (0, -1))
-DIAGONAL = ((1, 1), (1, -1), (-1, 1), (-1, -1))
 
 
 def halves(table):
@@ -71,7 +70,7 @@
 
     angle = 2 * np.pi * ((j[:, None] * j[None, :]) % 16) / 16
     both = np.stack([np.cos(angle), np.sin(angle)])
-    spread = np.einsum("pqj,xu,yv->pqxyvuj", both, np.eye(2), np.eye(8)).reshape(512, 256)
+    spread = np.einsum("pqj,yv->pqyvj", both, np.eye(8)).reshape(256, 128)
     y_second = np.concatenate(halves(spread), axis=0)
     return x_first, x_second, y_first, turn, y_second
 
@@ -104,9 +103,9 @@
 
 
 def kernel(
-    vx, vy, vz, owners, below, above, metric, x_first_in, x_second_in, y_first_in, turn_in,
+    vx, vy, vz, owners_in, below, above, metric, x_first_in, x_second_in, y_first_in, turn_in,
     y_second_in, out,
-    own, spread, ext, stress, flat, begun, source, outgoing, received, x_first, x_second, y_first, turn,
+    own, owners, spread, ext, stress, flat, begun, source, outgoing, received, x_first, x_second, y_first, turn,
     y_second, chosen, pivots, edges, edge_in, steps, steps_in, spectrum,
     in_sem, halo_send, halo_recv, all_send, all_recv, edge_send, edge_recv, own_sem, meeting,
 ):
@@ -117,7 +116,7 @@
 
     loads = [pltpu.make_async_copy(v, own.at[i], in_sem.at[i]) for i, v in enumerate((vx, vy, vz))]
     for index, (given, kept) in enumerate(
-        ((x_first_in, x_first), (x_second_in, x_second), (y_first_in, y_first), (turn_in, turn),
+        ((owners_in, owners), (x_first_in, x_first), (x_second_in, x_second), (y_first_in, y_first), (turn_in, turn),
          (y_second_in, y_second))
     ):
         loads.append(pltpu.make_async_copy(given, kept, in_sem.at[3 + index]))
@@ -126,7 +125,7 @@
 
     barrier = pltpu.get_barrier_semaphore()
 
-    for dz, dy in STRAIGHT + DIAGONAL:
+    for dz, dy in STRAIGHT:
         pl.semaphore_signal(barrier, inc=1, device_id=peer(dz, dy), device_id_type=MESH)
 
     for c in range(3):
@@ -140,7 +139,7 @@
                 ].astype(F32)
             ext[c, z + 2, 2:18] = spread[base : base + 256, :].reshape(16, 16, 128).astype(BF16)
 
-    pl.semaphore_wait(barrier, len(STRAIGHT) + len(DIAGONAL))
+    pl.semaphore_wait(barrier, len(STRAIGHT))
 
     def copy_to(index, dz, dy, given, kept):
         return pltpu.make_async_remote_copy(
@@ -177,7 +176,7 @@
         copy_to(12, 0, -1, (pl.ds(1, 1), rows(2, 2)), (pl.ds(1, 1), rows(18, 2))),
         copy_to(13, 0, -1, (pl.ds(4, 1), rows(2, 2)), (pl.ds(4, 1), rows(18, 2))),
     ]
-    for copy in near + rims + far:
+    for copy in near + rims:
         copy.start()
 
     def meet(number, peers):
@@ -185,7 +184,12 @@
             pl.semaphore_signal(meeting.at[number], inc=1, device_id=peer(dz, dy), device_id_type=MESH)
 
     meet(0, STRAIGHT)
-
+    pl.semaphore_wait(meeting.at[0], len(STRAIGHT))
+    for copy in far:
+        copy.start()
+    meet(1, ((0, 2), (0, -2)))
+
+    loads[3].wait()
     owner_row = owners[...]
     kx_row = mode_of(iota((1, KXR), 1))
     named = jnp.where(owner_row == iota((NGY, KXR), 0), 1.0, 0.0).astype(BF16)
@@ -196,10 +200,10 @@
     slot_row = jnp.sum(
         named * (rank + CAP * iota((NGY, KXR), 0).astype(F32)), axis=0, keepdims=True
     ).astype(I32)
-    for chi in range(2):
-        m = iota((512, 1), 0)
-        slot_id = (m // 8) * CAP + chi * 8 + m % 8
-        chosen[chi] = jnp.where(slot_row == slot_id, 1.0, 0.0).astype(BF16)
+    for k in range(4):
+        m = iota((256, 1), 0)
+        slot_id = (m // 4) * CAP + k * 4 + m % 4
+        chosen[k] = jnp.where(slot_row == slot_id, 1.0, 0.0).astype(BF16)
     mine = slot_row == gy * CAP + iota((CAP, KXR), 0)
     own_kx = jnp.sum(jnp.where(mine, kx_row.astype(F32), 0.0), axis=1, keepdims=True)
     own_ok = jnp.sum(jnp.where(mine, 1.0, 0.0), axis=1, keepdims=True)
@@ -207,8 +211,6 @@
     radius = own_kx * own_kx + ky * ky
     inside = jnp.where(radius <= float(KXR * KXR), 1.0, 0.0) * own_ok
 
-    pl.semaphore_wait(meeting.at[0], len(STRAIGHT))
-    meet(1, ((0, 2), (0, -2)))
 
     shift = BASE_SHIFT + MODE_SHIFT * (radius / float(KXR * KXR))
     for k in range(NZ):
@@ -362,7 +364,7 @@
             source[0, pl.ds(start, 32), z * 128 : (z + 1) * 128] = high
             source[1, pl.ds(start, 32), z * 128 : (z + 1) * 128] = low
 
-    for load in loads[3:]:
+    for load in loads[4:]:
         load.wait()
     high, low = source[0], source[1]
     first = dot(x_first[0], high) + dot(x_first[0], low) + dot(x_first[1], high)
@@ -393,13 +395,21 @@
     high, low = split(modes)
     modes = jnp.concatenate([high, low], 0)
     slots = []
-    for chi in range(2):
+    for k in range(4):
         taken = lax.dot_general(
-            chosen[chi], modes, (((1,), (1,)), ((), ())), preferred_element_type=F32
+            chosen[k], modes, (((1,), (1,)), ((), ())), preferred_element_type=F32
         )
         slots.append(taken + pltpu.roll(taken, 64, 1))
-    together = jnp.where(iota((512, 128), 1) < 64, slots[0], slots[1])
-    outgoing[...] = together.reshape(NGY, 8, 128)
+    front = iota((256, 128), 1) < 64
+    low, high = jnp.where(front, slots[0], slots[2]), jnp.where(front, slots[1], slots[3])
+    largest = jnp.max(jnp.maximum(jnp.abs(low), jnp.abs(high)), axis=0, keepdims=True)
+    exponent = jnp.ceil(jnp.log2(jnp.maximum(largest, 1e-30)) * 64.0) + 1.0
+    scale = 32767.0 * jnp.exp2(exponent * (-1.0 / 64.0))
+    low, high = (jnp.floor(v * scale + 0.5).astype(I32) for v in (low, high))
+    words = (high << 16) | (low & 0xFFFF)
+    for g in range(NGY):
+        outgoing[g, 0:4] = words[4 * g : 4 * g + 4]
+    outgoing[:, 4:5] = jnp.broadcast_to(exponent.astype(I32)[None], (NGY, 1, 128))
 
     pl.semaphore_wait(meeting.at[4], 2)
 
@@ -416,62 +426,26 @@
     @pl.loop(0, NGY - 1, unroll=3)
     def _(k):
         there = lax.rem(gy + NGY // 2 + (k + 1) // 2 * (1 - 2 * lax.rem(k, 2)) + NGY, NGY)
-        exchange(outgoing.at[there], received.at[gy], there).start()
-
-    keep = pltpu.make_async_copy(outgoing.at[gy], received.at[gy], own_sem)
+        exchange(outgoing.at[there, 0:5], received.at[gy, 0:5], there).start()
+
+    keep = pltpu.make_async_copy(outgoing.at[gy, 0:5], received.at[gy, 0:5], own_sem)
     keep.start()
     for copy in near + rims + far:
         copy.wait_send()
     keep.wait()
 
     others = pl.ds(0, NGY - 1)
-    exchange(outgoing.at[others], received.at[others], gy).wait()
-
-    pieces = []
+    exchange(outgoing.at[others, 0:5], received.at[others, 0:5], gy).wait()
+
+    low_level, high_level = DEPTH * gz, DEPTH * gz + 1
     arrived = received.reshape(NGY * 8, 128)
-    for clo in range(8):
-        turned = arrived[pl.ds(clo, NGY, stride=8), :].T
-        for chi in range(2):
-            real, imag = turned[64 * chi : 64 * chi + 32], turned[64 * chi + 32 : 64 * chi + 64]
-            pieces.append(jnp.concatenate([real, imag], 1))
-    left = jnp.concatenate(pieces, 0)
-    high, low = split(left)
-    both = dot(jnp.concatenate([high, low], 0), y_first[...])
-    value = both[0:512, 0:128] + both[512:1024, 0:128] + both[0:512, 128:256]
-    value = value.reshape(32, 16, 128)
-    swapped = pltpu.roll(value, 64, 2)
-    value = (value * turn[0] + swapped * turn[1]).reshape(16, 2, 16, 128)
-    right = jnp.concatenate([value[:, z].reshape(256, 128) for z in range(DEPTH)], 1)
-    high, low = split(right)
-    by_high = dot(y_second[...], high)
-    by_low = dot(y_second[0:512], low)
-    both = by_high[0:512] + by_high[512:1024] + by_low
-    sign = jnp.where(iota((256, 128), 1) < 64, 1.0, -1.0)
-    for z in range(DEPTH):
-        lanes = slice(128 * z, 128 * z + 128)
-        value = both[0:256, lanes] + pltpu.roll(both[256:512, lanes], 64, 1) * sign
-        front = iota((16, 128), 1) < 64
-        for pair in range(8):
-            one, two = value[32 * pair : 32 * pair + 16], value[32 * pair + 16 : 32 * pair + 32]
-            where = slice(128 * ((pair + 4) % 8), 128 * ((pair + 4) % 8) + 128)
-            kept = inside[:, where]
-            spectrum[0, z, :, where] = jnp.where(front, one, pltpu.roll(two, 64, 1)) * kept
-            spectrum[1, z, :, where] = jnp.where(front, pltpu.roll(one, 64, 1), two) * kept
-
-    low_level, high_level = DEPTH * gz, DEPTH * gz + 1
-    up = below[high_level] * pivots[2, low_level]
-    down = above[low_level] * pivots[3, high_level]
-    for side in range(2):
-        if side == 0:
-            values = [spectrum[part, 1] - up * spectrum[part, 0] for part in range(2)]
-        else:
-            values = [spectrum[part, 0] - down * spectrum[part, 1] for part in range(2)]
-        largest = jnp.maximum(jnp.abs(values[0]), jnp.abs(values[1]))
-        largest = jnp.maximum(jnp.max(largest, axis=1, keepdims=True), 1e-30)
-        scale = 32767.0 / largest
-        for part in range(2):
-            edges[side, part] = jnp.floor(values[part] * scale + 0.5).astype(I32).astype(jnp.int16)
-        steps[side] = jnp.broadcast_to(largest * (1.0 / 32767.0), (CAP, 128))
+    exponent = arrived[pl.ds(4, NGY, stride=8), :]
+    scale = jnp.exp2(exponent.astype(F32) * (1.0 / 64.0)) * (1.0 / 32767.0)
+    words = [arrived[pl.ds(c, NGY, stride=8), :] for c in range(4)]
+    turned = [(((w << 16) >> 16).astype(F32) * scale).T for w in words]
+    turned += [((w >> 16).astype(F32) * scale).T for w in words]
+    sign = jnp.where(iota((128, 128), 1) < 64, 1.0, -1.0)
+    front = iota((8, 128), 1) < 64
 
     def edge(d, given, kept, kind):
         there = lax.rem(gz + d, NGZ)
@@ -484,55 +458,107 @@
             device_id_type=MESH,
         )
 
-    crossing = [
-        edge(d, given, kept, kind)
-        for d in (2, 1, 3)
-        for kind, (given, kept) in enumerate(((edges, edge_in), (steps, steps_in)))
-    ]
-    for copy in crossing:
-        copy.start()
-    edge_in[gz] = jnp.zeros((2, CAP, NY), jnp.int16)
-    steps_in[gz] = jnp.zeros((CAP, 128), F32)
-
-    first_pivot, last_pivot = pivots[0, low_level], pivots[1, high_level]
-    cross_up, cross_down = below[high_level], above[low_level]
-    inverse = 1.0 / (first_pivot * last_pivot - cross_up * cross_down)
+    crossing = []
+    for chi in range(2):
+        mine = slice(8 * chi, 8 * chi + 8)
+        left = jnp.concatenate(
+            [
+                jnp.concatenate([t[64 * chi : 64 * chi + 32], t[64 * chi + 32 : 64 * chi + 64]], 1)
+                for t in turned
+            ],
+            0,
+        )
+        high, low = split(left)
+        both = dot(jnp.concatenate([high, low], 0), y_first[...])
+        value = both[0:256, 0:128] + both[256:512, 0:128] + both[0:256, 128:256]
+        value = value.reshape(16, 16, 128)
+        swapped = pltpu.roll(value, 64, 2)
+        value = (value * turn[0] + swapped * turn[1]).reshape(8, 2, 16, 128)
+        right = jnp.concatenate([value[:, z].reshape(128, 128) for z in range(DEPTH)], 1)
+        high, low = split(right)
+        by_high = dot(y_second[...], high)
+        by_low = dot(y_second[0:256], low)
+        both = by_high[0:256] + by_high[256:512] + by_low
+        for z in range(DEPTH):
+            lanes = slice(128 * z, 128 * z + 128)
+            value = both[0:128, lanes] + pltpu.roll(both[128:256, lanes], 64, 1) * sign
+            for pair in range(8):
+                one, two = value[16 * pair : 16 * pair + 8], value[16 * pair + 8 : 16 * pair + 16]
+                where = slice(128 * ((pair + 4) % 8), 128 * ((pair + 4) % 8) + 128)
+                kept = inside[mine, where]
+                spectrum[0, z, mine, where] = jnp.where(front, one, pltpu.roll(two, 64, 1)) * kept
+                spectrum[1, z, mine, where] = jnp.where(front, pltpu.roll(one, 64, 1), two) * kept
+
+        up = below[high_level] * pivots[2, low_level, mine]
+        down = above[low_level] * pivots[3, high_level, mine]
+        for side in range(2):
+            near_level, far_level, weight = (1, 0, up) if side == 0 else (0, 1, down)
+            values = [
+                spectrum[part, near_level, mine] - weight * spectrum[part, far_level, mine]
+                for part in range(2)
+            ]
+            largest = jnp.maximum(jnp.abs(values[0]), jnp.abs(values[1]))
+            largest = jnp.maximum(jnp.max(largest, axis=1, keepdims=True), 1e-30)
+            scale = 32767.0 / largest
+            codes = jnp.concatenate([jnp.floor(v * scale + 0.5).astype(I32) for v in values], 0)
+            edges[chi, side] = codes.astype(jnp.int16)
+            steps[chi, side] = jnp.broadcast_to(largest * (1.0 / 32767.0), (8, 128))
+        copies = [
+            edge(d, given.at[chi], kept.at[chi], 2 * chi + kind)
+            for d in (2, 1, 3)
+            for kind, (given, kept) in enumerate(((edges, edge_in), (steps, steps_in)))
+        ]
+        for copy in copies:
+            copy.start()
+        edge_in[chi, gz] = jnp.zeros((16, NY), jnp.int16)
+        steps_in[chi, gz] = jnp.zeros((8, 128), F32)
+        crossing.append(copies)
+
     beneath = jnp.maximum(low_level - 1, 0)
     over = jnp.minimum(high_level + 1, NZ - 1)
-    from_below = below[low_level] * pivots[2, beneath]
-    from_above = above[high_level] * pivots[3, over]
-    for copy in crossing:
-        copy.wait()
-
-    def edge_of(block, part):
-        step = jnp.concatenate([steps_in[block]] * (NY // 128), 1)
-        return edge_in[block, part].astype(I32).astype(F32) * step
-
-    for part in range(2):
-        reached = jnp.zeros((CAP, NY), F32)
-        for block in range(NGZ - 1):
-            new = edge_of(block, part)
-            if block > 0:
-                k = DEPTH * block
-                new = new + (below[k] * below[k + 1]) * pivots[2, k - 1] * pivots[2, k] * reached
-            reached = jnp.where(block < gz, new, reached)
-        lower = spectrum[part, 0] - from_below * reached
-        reached = jnp.zeros((CAP, NY), F32)
-        for block in range(NGZ - 1, 0, -1):
-            new = edge_of(block, part)
-            if block < NGZ - 1:
-                k = DEPTH * block
-                new = new + (above[k] * above[k + 1]) * pivots[3, k + 1] * pivots[3, k + 2] * reached
-            reached = jnp.where(block > gz, new, reached)
-        upper = spectrum[part, 1] - from_above * reached
-        for z, value in enumerate(
-            (last_pivot * lower - cross_down * upper, first_pivot * upper - cross_up * lower)
-        ):
-            value = value * inverse
-            for tile in range(NY // 128):
-                out[pl.ds(part * 16 + tile * 2 + z, CAP, stride=32), :] = value[
-                    :, tile * 128 : (tile + 1) * 128
-                ]
+    cross_up, cross_down = below[high_level], above[low_level]
+    for chi in range(2):
+        mine = slice(8 * chi, 8 * chi + 8)
+        first_pivot, last_pivot = pivots[0, low_level, mine], pivots[1, high_level, mine]
+        inverse = 1.0 / (first_pivot * last_pivot - cross_up * cross_down)
+        from_below = below[low_level] * pivots[2, beneath, mine]
+        from_above = above[high_level] * pivots[3, over, mine]
+        for copy in crossing[chi]:
+            copy.wait()
+
+        def edges_of(block):
+            step = jnp.concatenate([steps_in[chi, block]] * (NY // 128), 1)
+            codes = edge_in[chi, block].astype(I32).astype(F32)
+            return codes[0:8] * step, codes[8:16] * step
+
+        arriving = [edges_of(block) for block in range(NGZ)]
+        for part in range(2):
+            reached = jnp.zeros((8, NY), F32)
+            for block in range(NGZ - 1):
+                new = arriving[block][part]
+                if block > 0:
+                    k = DEPTH * block
+                    along = pivots[2, k - 1, mine] * pivots[2, k, mine]
+                    new = new + (below[k] * below[k + 1]) * along * reached
+                reached = jnp.where(block < gz, new, reached)
+            lower = spectrum[part, 0, mine] - from_below * reached
+            reached = jnp.zeros((8, NY), F32)
+            for block in range(NGZ - 1, 0, -1):
+                new = arriving[block][part]
+                if block < NGZ - 1:
+                    k = DEPTH * block
+                    along = pivots[3, k + 1, mine] * pivots[3, k + 2, mine]
+                    new = new + (above[k] * above[k + 1]) * along * reached
+                reached = jnp.where(block > gz, new, reached)
+            upper = spectrum[part, 1, mine] - from_above * reached
+            for z, value in enumerate(
+                (last_pivot * lower - cross_down * upper, first_pivot * upper - cross_up * lower)
+            ):
+                value = value * inverse
+                for tile in range(NY // 128):
+                    out[pl.ds(256 * chi + part * 16 + tile * 2 + z, 8, stride=32), :] = value[
+                        :, tile * 128 : (tile + 1) * 128
+                    ]
 
 
 def per_device(velocity_x, velocity_y, velocity_z, owners, below, above, metric):
@@ -543,29 +569,30 @@
     result = pl.pallas_call(
         kernel,
         out_shape=pltpu.VMEM((2 * DEPTH * CAP * NY // 128, 128), F32),
-        in_specs=[anywhere] * 3 + [pl.BlockSpec(memory_space=pltpu.VMEM)] + [scalars] * 3 + [anywhere] * 5,
+        in_specs=[anywhere] * 4 + [scalars] * 3 + [anywhere] * 5,
         out_specs=pl.BlockSpec(memory_space=pltpu.VMEM),
         scratch_shapes=[
             pltpu.VMEM((3, DEPTH, ROWS, NX), BF16),
+            pltpu.VMEM((1, KXR), I32),
             pltpu.VMEM((3 * DEPTH * ROWS * 16, 128), F32),
             pltpu.VMEM((3, 6, 20, 16, 128), BF16),
             pltpu.VMEM((6, 4, 18, 16, 128), F32),
             pltpu.VMEM((3, 2, 18, 16, 128), F32),
             pltpu.VMEM((DEPTH, ROWS, 16, 128), F32),
             pltpu.VMEM((2, 256, 256), BF16),
-            pltpu.VMEM((NGY, 8, 128), F32),
-            pltpu.VMEM((NGY, 8, 128), F32),
+            pltpu.VMEM((NGY, 8, 128), I32),
+            pltpu.VMEM((NGY, 8, 128), I32),
         ]
         + [pltpu.VMEM(c.shape, c.dtype) for c in consts]
         + [
-            pltpu.VMEM((2, 512, KXR), BF16),
+            pltpu.VMEM((4, 256, KXR), BF16),
             pltpu.VMEM((4, NZ, CAP, NY), F32),
-            pltpu.VMEM((2, 2, CAP, NY), jnp.int16),
-            pltpu.VMEM((NGZ, 2, CAP, NY), jnp.int16),
-            pltpu.VMEM((2, CAP, 128), F32),
-            pltpu.VMEM((NGZ, CAP, 128), F32),
+            pltpu.VMEM((2, 2, 16, NY), jnp.int16),
+            pltpu.VMEM((2, NGZ, 16, NY), jnp.int16),
+            pltpu.VMEM((2, 2, 8, 128), F32),
+            pltpu.VMEM((2, NGZ, 8, 128), F32),
             pltpu.VMEM((2, DEPTH, CAP, NY), F32),
-            dma((8,)), dma((14,)), dma((14,)), dma(()), dma(()), dma((2, NGZ)), dma((2, NGZ)),
+            dma((9,)), dma((14,)), dma((14,)), dma(()), dma(()), dma((4, NGZ)), dma((4, NGZ)),
             dma(()),
             pltpu.SemaphoreType.REGULAR((5,)),
         ],

time: 42.5 us -> 40.6 us (0.955)
  Pallas kernels: 41.7 us -> 39.8 us
    pallas_call x1, Pallas kernels: 41.7 us -> 39.8 us  [per_device(): pl.pallas_call(kernel, out_shape=pltpu.VMEM((2 * DEPTH * CAP * NY // 128,...]
where the time goes in v4:
time: 40.6 us; the launch traced here: 40.5 us
  Pallas kernels  39.8 us (98%)
  local copies, waits for them, and re-layouts  0.71 us (2%)
    pallas_call x1, Pallas kernels, per_device(): pl.pallas_call(kernel, out_shape=pltpu.VMEM((2 * DEPTH * CAP * NY // 128,...  39.8 us

profile of v4, /device:TPU:1, one launch (start us, length us, event | category | flops | bytes accessed | tf_op | source)
XLA Modules:
  0.0 40.5 jit_solution(12108645702766738066)
XLA Ops:
  0.0 39.8 %shard_map.118 = f32[512,128]{1,0:T(8,128)S(1)} custom-call(bf16[2,16,2048]{2,1,0:T(8,128)(2,1)} %vx.1, bf16[2,16,2048]{2,1,0:T(8,128)(2,1)} %vy.1, bf16[2,16,2048]{2,1,0:T(8,128)(2,1)} %vz.1, s32[1,512]{1,0:T(1,128)} %bitcast.7, f32[8]{0:T(128)} %below.1, f32[8]{0:T(128)} %above.1, f32[8]{0:T(128)} %metric.1, ...), custom_call_target="tpu_custom_call" | custom-call | tf_op jit(solution)/shard_map/pallas_call | solution.py:569
  39.8 0.7 %copy.15 = f32[1,16,2,2,1024]{4,3,2,1,0:T(2,128)} copy(f32[1,16,2,2,1024]{4,3,2,1,0:T(2,128)S(1)} %bitcast.6) | data formatting | bytes 524288

commit v5 on v4

--- a/solution.py
+++ b/solution.py
@@ -258,12 +258,14 @@
     def slopes_z(level, row, count):
         return [(at(c, level + 1, row, count) - at(c, level - 1, row, count)) * 0.5 for c in range(3)]
 
-    for copy in near:
-        copy.wait_recv()
+    near[0].wait_recv()
     zero_level(0, 1, 2, 16)
+    corners[0].start()
+    corners[2].start()
+    near[1].wait_recv()
     zero_level(NGZ - 1, 4, 2, 16)
-    for copy in corners:
-        copy.start()
+    corners[1].start()
+    corners[3].start()
     for copy in rims + corners:
         copy.wait_recv()
     for copy in corners:
@@ -272,7 +274,7 @@
     zero_level(NGZ - 1, 4, 0, 20)
     zero_rim((1, 2, 3, 4))
 
-    @pl.loop(0, 18, unroll=3)
+    @pl.loop(0, 18, unroll=6)
     def _(step):
         level, row, count = 2 + step // 9, 1 + 2 * lax.rem(step, 9), 2
         dx, dy = flat_slopes(level, row, count)
@@ -292,7 +294,7 @@
     pl.semaphore_wait(meeting.at[2], 2)
     meet(3, ((0, 8), (0, -8)))
 
-    @pl.loop(0, 18, unroll=3)
+    @pl.loop(0, 18, unroll=6)
     def _(step):
         side, row, count = step // 9, 1 + 2 * lax.rem(step, 9), 2
         dx, dy = flat_slopes(1 + 3 * side, row, count)
@@ -303,7 +305,7 @@
 
     for z in range(DEPTH):
 
-        @pl.loop(0, 8, unroll=4)
+        @pl.loop(0, 8, unroll=8)
         def _(step):
             row = 2 * step
             sign = 1.0 if z == 0 else -1.0
@@ -333,7 +335,7 @@
     zero_level(NGZ - 1, 5, 0, 20)
     zero_rim((0, 5))
 
-    @pl.loop(0, 18, unroll=3)
+    @pl.loop(0, 18, unroll=6)
     def _(step):
         side, row, count = step // 9, 1 + 2 * lax.rem(step, 9), 2
         level = 1 + 3 * side
@@ -347,7 +349,7 @@
 
     for z in range(DEPTH):
 
-        @pl.loop(0, 8, unroll=4)
+        @pl.loop(0, 8, unroll=8)
         def _(step):
             row = 2 * step
             sign = -1.0 if z == 0 else 1.0
@@ -423,9 +425,17 @@
             device_id_type=MESH,
         )
 
+    def away(half, k):
+        return half + (k + 1) // 2 * (1 - 2 * lax.rem(k, 2))
+
     @pl.loop(0, NGY - 1, unroll=3)
     def _(k):
-        there = lax.rem(gy + NGY // 2 + (k + 1) // 2 * (1 - 2 * lax.rem(k, 2)) + NGY, NGY)
+        step_z, step_y = away(4, lax.rem(k // 2, 8)), away(2, k // 16)
+        there = (
+            lax.rem(gy // 8 + step_z, 8) * 8
+            + lax.rem(lax.rem(gy // 2, 4) + step_y, 4) * 2
+            + lax.rem(gy + 1 + k, 2)
+        )
         exchange(outgoing.at[there, 0:5], received.at[gy, 0:5], there).start()
 
     keep = pltpu.make_async_copy(outgoing.at[gy, 0:5], received.at[gy, 0:5], own_sem)
@@ -505,7 +515,7 @@
             steps[chi, side] = jnp.broadcast_to(largest * (1.0 / 32767.0), (8, 128))
         copies = [
             edge(d, given.at[chi], kept.at[chi], 2 * chi + kind)
-            for d in (2, 1, 3)
+            for d in (1, 3, 2)
             for kind, (given, kept) in enumerate(((edges, edge_in), (steps, steps_in)))
         ]
         for copy in copies:

time: 40.6 us -> 39.4 us (0.970)
  Pallas kernels: 39.8 us -> 38.5 us
    pallas_call x1, Pallas kernels: 39.8 us -> 38.5 us  [per_device(): pl.pallas_call(kernel, out_shape=pltpu.VMEM((2 * DEPTH * CAP * NY // 128,...]
where the time goes in v5:
time: 39.4 us; the launch traced here: 39.3 us
  Pallas kernels  38.5 us (98%)
  local copies, waits for them, and re-layouts  0.71 us (2%)
    pallas_call x1, Pallas kernels, per_device(): pl.pallas_call(kernel, out_shape=pltpu.VMEM((2 * DEPTH * CAP * NY // 128,...  38.5 us

profile of v5, /device:TPU:1, one launch (start us, length us, event | category | flops | bytes accessed | tf_op | source)
XLA Modules:
  0.0 39.3 jit_solution(12185303888303808475)
XLA Ops:
  0.0 38.5 %shard_map.118 = f32[512,128]{1,0:T(8,128)S(1)} custom-call(bf16[2,16,2048]{2,1,0:T(8,128)(2,1)} %vx.1, bf16[2,16,2048]{2,1,0:T(8,128)(2,1)} %vy.1, bf16[2,16,2048]{2,1,0:T(8,128)(2,1)} %vz.1, s32[1,512]{1,0:T(1,128)} %bitcast.7, f32[8]{0:T(128)} %below.1, f32[8]{0:T(128)} %above.1, f32[8]{0:T(128)} %metric.1, ...), custom_call_target="tpu_custom_call" | custom-call | tf_op jit(solution)/shard_map/pallas_call | solution.py:579
  38.6 0.7 %copy.15 = f32[1,16,2,2,1024]{4,3,2,1,0:T(2,128)} copy(f32[1,16,2,2,1024]{4,3,2,1,0:T(2,128)S(1)} %bitcast.6) | data formatting | bytes 524288

commit v6 on v5

--- a/solution.py
+++ b/solution.py
@@ -114,19 +114,19 @@
     def peer(dz, dy):
         return (lax.rem(gz + dz + NGZ, NGZ), lax.rem(gy + dy + NGY, NGY))
 
+    barrier = pltpu.get_barrier_semaphore()
+
+    for dz, dy in STRAIGHT:
+        pl.semaphore_signal(barrier, inc=1, device_id=peer(dz, dy), device_id_type=MESH)
+
     loads = [pltpu.make_async_copy(v, own.at[i], in_sem.at[i]) for i, v in enumerate((vx, vy, vz))]
     for index, (given, kept) in enumerate(
         ((owners_in, owners), (x_first_in, x_first), (x_second_in, x_second), (y_first_in, y_first), (turn_in, turn),
          (y_second_in, y_second))
     ):
         loads.append(pltpu.make_async_copy(given, kept, in_sem.at[3 + index]))
-    for load in loads:
+    for load in loads[:4]:
         load.start()
-
-    barrier = pltpu.get_barrier_semaphore()
-
-    for dz, dy in STRAIGHT:
-        pl.semaphore_signal(barrier, inc=1, device_id=peer(dz, dy), device_id_type=MESH)
 
     for c in range(3):
         loads[c].wait()
@@ -178,6 +178,8 @@
     ]
     for copy in near + rims:
         copy.start()
+    for load in loads[4:]:
+        load.start()
 
     def meet(number, peers):
         for dz, dy in peers:

time: 39.4 us -> 39.4 us (level)
  no operation moved by 1% of the time
where the time goes in v6:
time: 39.4 us; the launch traced here: 39.3 us
  Pallas kernels  38.5 us (98%)
  local copies, waits for them, and re-layouts  0.71 us (2%)
    pallas_call x1, Pallas kernels, per_device(): pl.pallas_call(kernel, out_shape=pltpu.VMEM((2 * DEPTH * CAP * NY // 128,...  38.5 us

profile of v6, /device:TPU:1, one launch (start us, length us, event | category | flops | bytes accessed | tf_op | source)
XLA Modules:
  0.0 39.3 jit_solution(13769911373531758985)
XLA Ops:
  0.0 38.5 %shard_map.118 = f32[512,128]{1,0:T(8,128)S(1)} custom-call(bf16[2,16,2048]{2,1,0:T(8,128)(2,1)} %vx.1, bf16[2,16,2048]{2,1,0:T(8,128)(2,1)} %vy.1, bf16[2,16,2048]{2,1,0:T(8,128)(2,1)} %vz.1, s32[1,512]{1,0:T(1,128)} %bitcast.7, f32[8]{0:T(128)} %below.1, f32[8]{0:T(128)} %above.1, f32[8]{0:T(128)} %metric.1, ...), custom_call_target="tpu_custom_call" | custom-call | tf_op jit(solution)/shard_map/pallas_call | solution.py:581
  38.6 0.7 %copy.15 = f32[1,16,2,2,1024]{4,3,2,1,0:T(2,128)} copy(f32[1,16,2,2,1024]{4,3,2,1,0:T(2,128)S(1)} %bitcast.6) | data formatting | bytes 524288
